TPU v7x, 768 devices: a whole 4x8x12 slice. The times are simulated.
768 devices in a mesh: section: 12 (over z_lo, core), tp: 16 (over z_hi, y), dp: 4 (over x).
Axes of the slice: x: 4, y: 8, z: 12 (z_hi: 2, z_lo: 6; z = z_hi * 6 + z_lo), core: 2. Of those that a mesh axis runs over, the one named last changes fastest.
Arguments:
- attn_out: bfloat16 [12, 1024, 8192], P('section', 'dp', 'tp'), may hold values from -6 to 6
- dest: int32 [1024, 1], P('dp'), may hold values from 0 to 3; in each aligned block of 256 rows (0 to 255, 256 to 511, ...) at most 128 rows name the same one
- o_weight: bfloat16 [12, 8192, 8192], P('section', 'tp'), may hold values from -0.0625 to 0.0625
- head: bfloat16 [12, 8192], P('section'), may hold values from -0.0625 to 0.0625
- coef: float32 [12], P('section'), may hold values from 0.5 to 1.5
Outputs:
- advantage: float32 [1024], P('dp')
Inputs may be any that keep to these rules, and one draw needn't show every extreme that they name: `dest`: among the tokens of one index of dp, at most 128 have one value; every value 0 to 3 occurs among all 1024 tokens.
All inputs are finite; a program needn't handle non-finite values.
Results may differ from a plain program's by a relative error of at most 0.0003.
Values sent between devices are 32-bit elements; how exact they have to be, the bound alone decides.
No kernel may reach another device: no remote copies, remote signals or barrier semaphores. Data moves between devices by JAX's collectives and lax.ppermute only.
A program may use at most 64 MiB of HBM per device.

v0:
```python
import jax
import jax.numpy as jnp
from jax import lax
from jax.sharding import Mesh, PartitionSpec as P


ZH = 2
SPLITS = (4096, 4096)
LANES = 128


def everyone(value, axes):
    members = lax.axis_size(axes)
    padded = jnp.pad(value, (0, LANES - value.shape[0]))
    copies = jnp.broadcast_to(padded[None, :], (members, LANES))
    return lax.all_to_all(copies, axes, 0, 0, tiled=True)


def body(attn_out, dest, o_weight, head, coef):
    rows = attn_out[0]
    matrix = o_weight[0]
    tokens, width = rows.shape[0], matrix.shape[1]
    zh, y = lax.axis_index("zh"), lax.axis_index("y")
    ring, groups = lax.axis_size("y"), lax.axis_size("dp")
    own = tokens // (ring * ZH)
    far = ring // 2
    swap = [(i, (i + 1) % ZH) for i in range(ZH)]

    sent = []

    def join(*values):
        total = values[0]
        for value in values[1:]:
            total = total + value
        return total

    def ship(value, axis, pairs):
        sent.append(value)
        return lax.ppermute(value, axis, pairs)

    def along(value, by):
        return ship(value, "y", [(i, (i + by) % ring) for i in range(ring)])

    def after_last(value):
        return lax.optimization_barrier((value, sent[-1]))[0] if sent else value

    cuts = [0]
    for columns in SPLITS:
        cuts.append(cuts[-1] + columns)
    spans = range(len(SPLITS))
    parts, ups, downs = [], [], []

    def owned_by(g, owner):
        return lax.dynamic_index_in_dim(parts[g], owner % ring, 0, False)

    for g in spans:
        product = jnp.dot(after_last(rows), matrix[:, cuts[g] : cuts[g + 1]], preferred_element_type=jnp.float32)
        parts.append(product.reshape(ring, ZH, own, SPLITS[g]))
        opposite = owned_by(g, y + far)
        ups.append(along(opposite[0], 1)[None])
        downs.append(along(opposite[1], -1)[None])
    for step in range(far - 1, 0, -1):
        for g in spans:
            up = after_last(ups[g])
            if step == far - 1:
                up = lax.pad(up, 0.0, ((0, 1, 0), (0, 0, 0), (0, 0, 0)))
            ups[g] = along(join(owned_by(g, y + step), up), 1)
            down = after_last(downs[g])
            if step == far - 1:
                down = lax.pad(down, 0.0, ((1, 0, 0), (0, 0, 0), (0, 0, 0)))
            downs[g] = along(join(owned_by(g, y - step), down), -1)

    gain = head[0].astype(jnp.float32)
    squares, numer = 0.0, 0.0
    for g in spans:
        total = join(owned_by(g, y), after_last(ups[g]), downs[g])
        kept = jnp.where(zh == 0, total[0], total[1])
        given = jnp.where(zh == 0, total[1], total[0])
        full = kept + ship(given, "zh", swap)
        squares = squares + jnp.sum(full * full, axis=1)
        numer = numer + jnp.sum(full * gain[None, cuts[g] : cuts[g + 1]], axis=1)
    score = coef[0] * numer * lax.rsqrt(squares / width + 1e-05)

    names = jnp.arange(groups, dtype=jnp.int32)[None, :]
    target = dest[:, 0]
    own_target = lax.dynamic_slice_in_dim(target, (y * ZH + zh) * own, own)
    own_member = (own_target[:, None] == names).astype(jnp.float32)
    combined = jnp.sum(everyone(score, "section"), axis=0)[:own]
    totals = jnp.sum(own_member * combined[:, None], axis=0)
    counts = jnp.sum(own_member, axis=0)
    pieces = everyone(jnp.concatenate([combined, totals, counts]), ("dp", "y", "zh"))
    pieces = pieces.reshape(groups, ring * ZH, LANES)
    mine = lax.dynamic_index_in_dim(pieces, lax.axis_index("dp"), 0, False)[:, :own].reshape(tokens)
    tail = jnp.sum(pieces[:, :, own : own + 2 * groups], axis=(0, 1))
    group_mean = tail[:groups] / tail[groups:]
    member = (target[:, None] == names).astype(jnp.float32)
    return mine - jnp.sum(member * group_mean[None, :], axis=1)


def solution(mesh):
    sizes = mesh.shape
    split = Mesh(
        mesh.devices.reshape(sizes["section"], ZH, sizes["tp"] // ZH, sizes["dp"]), ("section", "zh", "y", "dp")
    )
    features = ("zh", "y")
    placed = (
        P("section", "dp", features),
        P("dp", None),
        P("section", features, None),
        P("section", None),
        P("section"),
    )

    return jax.shard_map(body, mesh=split, in_specs=placed, out_specs=P("dp"), check_vma=False)
```

profile of v0, /device:TPU:1, one launch (start us, length us, event | category | flops | bytes accessed | tf_op | source)
XLA Modules:
  0.0 186.6 jit_solution(17412542642154116221)
XLA Ops:
  0.0 0.9 copy-done
  1.0 3.6 %fusion.2 = f32[8,2,16,4096]{3,2,1,0:T(8,128)S(1)} fusion(bf16[8,2,16,512]{3,2,1,0:T(8,128)(2,1)S(1)} %bitcast.75, bf16[512,8192]{1,0:T(8,128)(2,1)} %bitcast.85), kind=kOutput, calls=%fused_computation.3 | convolution fusion | flops 1073741824 | bytes 8650752 | tf_op jit(solution)/shard_map/dot_general | solution.py:57
  4.6 4.2 %collective-permute-start = (f32[16,4096]{1,0:T(8,128)S(1)}, f32[16,4096]{1,0:T(8,128)S(1)}, u32[]{:S(2)}, u32[]{:S(2)}) collective-permute-start(f32[16,4096]{1,0:T(8,128)S(1)} %get-tuple-element.43), channel_id=1, source_target_pairs={{0,4},{4,8},{8,12},{12,16},{16,20},{20,24},{24,28},{28,0},{1,5},{5... | collective-permute-start | bytes 786440 | tf_op jit(solution)/shard_map/ppermute | solution.py:39
  8.8 3.8 %collective-permute-start.4 = (f32[16,4096]{1,0:T(8,128)S(1)}, f32[16,4096]{1,0:T(8,128)S(1)}, u32[]{:S(2)}, u32[]{:S(2)}) collective-permute-start(f32[16,4096]{1,0:T(8,128)S(1)} %get-tuple-element.44), channel_id=1, source_target_pairs={{0,28},{4,0},{8,4},{12,8},{16,12},{20,16},{24,20},{28,24},{1,29},{... | collective-permute-start | bytes 786440 | tf_op jit(solution)/shard_map/ppermute | solution.py:39
  12.6 1.3 fusion
  13.9 2.0 %copy-done.1 = f32[256,4096]{1,0:T(8,128)} copy-done((f32[256,4096]{1,0:T(8,128)}, f32[256,4096]{1,0:T(8,128)S(1)}, u32[]{:S(2)}) %copy-start.1) | copy-done | bytes 4194328
  15.9 1.9 %collective-permute-start.3 = (f32[16,4096]{1,0:T(8,128)S(1)}, f32[16,4096]{1,0:T(8,128)S(1)}, u32[]{:S(2)}, u32[]{:S(2)}) collective-permute-start(f32[16,4096]{1,0:T(8,128)S(1)} %get-tuple-element.41), channel_id=1, source_target_pairs={{0,4},{4,8},{8,12},{12,16},{16,20},{20,24},{24,28},{28,0},{1,5},{5... | collective-permute-start | bytes 786440 | tf_op jit(solution)/shard_map/ppermute | solution.py:39
  17.9 4.6 %collective-permute-start.2 = (f32[16,4096]{1,0:T(8,128)S(1)}, f32[16,4096]{1,0:T(8,128)S(1)}, u32[]{:S(2)}, u32[]{:S(2)}) collective-permute-start(f32[16,4096]{1,0:T(8,128)S(1)} %get-tuple-element.42), channel_id=1, source_target_pairs={{0,28},{4,0},{8,4},{12,8},{16,12},{20,16},{24,20},{28,24},{1,29},{... | collective-permute-start | bytes 786440 | tf_op jit(solution)/shard_map/ppermute | solution.py:39
  22.6 1.2 bitcast_add_fusion.10
  23.9 2.2 %collective-permute-start.1 = (f32[2,16,4096]{2,1,0:T(8,128)S(1)}, f32[2,16,4096]{2,1,0:T(8,128)S(1)}, u32[]{:S(2)}, u32[]{:S(2)}) collective-permute-start(f32[2,16,4096]{2,1,0:T(8,128)S(1)} %bitcast_add_fusion.10), channel_id=1, source_target_pairs={{0,4},{4,8},{8,12},{12,16},{16,20},{20,24},{24,28},{28,0},{1,5},{5... | collective-permute-start | bytes 1572872 | tf_op jit(solution)/shard_map/ppermute | solution.py:39
  26.1 1.1 bitcast_add_fusion.7
  27.1 4.6 %collective-permute-start.8 = (f32[2,16,4096]{2,1,0:T(8,128)S(1)}, f32[2,16,4096]{2,1,0:T(8,128)S(1)}, u32[]{:S(2)}, u32[]{:S(2)}) collective-permute-start(f32[2,16,4096]{2,1,0:T(8,128)S(1)} %bitcast_add_fusion.7), channel_id=1, source_target_pairs={{0,28},{4,0},{8,4},{12,8},{16,12},{20,16},{24,20},{28,24},{1,29},{... | collective-permute-start | bytes 1572872 | tf_op jit(solution)/shard_map/ppermute | solution.py:39
  31.7 1.1 bitcast_add_fusion.8
  32.8 1.9 %collective-permute-start.7 = (f32[2,16,4096]{2,1,0:T(8,128)S(1)}, f32[2,16,4096]{2,1,0:T(8,128)S(1)}, u32[]{:S(2)}, u32[]{:S(2)}) collective-permute-start(f32[2,16,4096]{2,1,0:T(8,128)S(1)} %bitcast_add_fusion.8), channel_id=1, source_target_pairs={{0,4},{4,8},{8,12},{12,16},{16,20},{20,24},{24,28},{28,0},{1,5},{5... | collective-permute-start | bytes 1572872 | tf_op jit(solution)/shard_map/ppermute | solution.py:39
  34.8 1.1 bitcast_add_fusion.9
  35.9 4.6 %collective-permute-start.6 = (f32[2,16,4096]{2,1,0:T(8,128)S(1)}, f32[2,16,4096]{2,1,0:T(8,128)S(1)}, u32[]{:S(2)}, u32[]{:S(2)}) collective-permute-start(f32[2,16,4096]{2,1,0:T(8,128)S(1)} %bitcast_add_fusion.9), channel_id=1, source_target_pairs={{0,28},{4,0},{8,4},{12,8},{16,12},{20,16},{24,20},{28,24},{1,29},{... | collective-permute-start | bytes 1572872 | tf_op jit(solution)/shard_map/ppermute | solution.py:39
  40.5 1.9 %collective-permute-start.5 = (f32[2,16,4096]{2,1,0:T(8,128)S(1)}, f32[2,16,4096]{2,1,0:T(8,128)S(1)}, u32[]{:S(2)}, u32[]{:S(2)}) collective-permute-start(f32[2,16,4096]{2,1,0:T(8,128)S(1)} %bitcast_add_fusion.11), channel_id=1, source_target_pairs={{0,4},{4,8},{8,12},{12,16},{16,20},{20,24},{24,28},{28,0},{1,5},{5... | collective-permute-start | bytes 1572872 | tf_op jit(solution)/shard_map/ppermute | solution.py:39
  42.5 4.6 %collective-permute-start.12 = (f32[2,16,4096]{2,1,0:T(8,128)S(1)}, f32[2,16,4096]{2,1,0:T(8,128)S(1)}, u32[]{:S(2)}, u32[]{:S(2)}) collective-permute-start(f32[2,16,4096]{2,1,0:T(8,128)S(1)} %bitcast_add_fusion.4), channel_id=1, source_target_pairs={{0,28},{4,0},{8,4},{12,8},{16,12},{20,16},{24,20},{28,24},{1,29},{... | collective-permute-start | bytes 1572872 | tf_op jit(solution)/shard_map/ppermute | solution.py:39
  47.1 0.8 collective-permute-done.7
  48.0 1.9 %collective-permute-start.11 = (f32[2,16,4096]{2,1,0:T(8,128)S(1)}, f32[2,16,4096]{2,1,0:T(8,128)S(1)}, u32[]{:S(2)}, u32[]{:S(2)}) collective-permute-start(f32[2,16,4096]{2,1,0:T(8,128)S(1)} %bitcast_add_fusion.5), channel_id=1, source_target_pairs={{0,4},{4,8},{8,12},{12,16},{16,20},{20,24},{24,28},{28,0},{1,5},{5... | collective-permute-start | bytes 1572872 | tf_op jit(solution)/shard_map/ppermute | solution.py:39
  50.0 5.3 %collective-permute-start.10 = (f32[2,16,4096]{2,1,0:T(8,128)S(1)}, f32[2,16,4096]{2,1,0:T(8,128)S(1)}, u32[]{:S(2)}, u32[]{:S(2)}) collective-permute-start(f32[2,16,4096]{2,1,0:T(8,128)S(1)} %bitcast_add_fusion.6), channel_id=1, source_target_pairs={{0,28},{4,0},{8,4},{12,8},{16,12},{20,16},{24,20},{28,24},{1,29},{... | collective-permute-start | bytes 1572872 | tf_op jit(solution)/shard_map/ppermute | solution.py:39
  55.3 3.8 %collective-permute-done.5 = f32[2,16,4096]{2,1,0:T(8,128)S(1)} collective-permute-done((f32[2,16,4096]{2,1,0:T(8,128)S(1)}, f32[2,16,4096]{2,1,0:T(8,128)S(1)}, u32[]{:S(2)}, u32[]{:S(2)}) %collective-permute-start.5) | collective-permute-done | bytes 524320 | tf_op jit(solution)/shard_map/ppermute | solution.py:39
  59.2 1.9 %collective-permute-start.9 = (f32[2,16,4096]{2,1,0:T(8,128)S(1)}, f32[2,16,4096]{2,1,0:T(8,128)S(1)}, u32[]{:S(2)}, u32[]{:S(2)}) collective-permute-start(f32[2,16,4096]{2,1,0:T(8,128)S(1)} %bitcast_add_fusion.12), channel_id=1, source_target_pairs={{0,4},{4,8},{8,12},{12,16},{16,20},{20,24},{24,28},{28,0},{1,5},{5... | collective-permute-start | bytes 1572872 | tf_op jit(solution)/shard_map/ppermute | solution.py:39
  61.2 5.3 %collective-permute-start.13 = (f32[2,16,4096]{2,1,0:T(8,128)S(1)}, f32[2,16,4096]{2,1,0:T(8,128)S(1)}, u32[]{:S(2)}, u32[]{:S(2)}) collective-permute-start(f32[2,16,4096]{2,1,0:T(8,128)S(1)} %bitcast_add_fusion.1), channel_id=1, source_target_pairs={{0,28},{4,0},{8,4},{12,8},{16,12},{20,16},{24,20},{28,24},{1,29},{... | collective-permute-start | bytes 1572872 | tf_op jit(solution)/shard_map/ppermute | solution.py:39
  66.5 3.8 %collective-permute-done.11 = f32[2,16,4096]{2,1,0:T(8,128)S(1)} collective-permute-done((f32[2,16,4096]{2,1,0:T(8,128)S(1)}, f32[2,16,4096]{2,1,0:T(8,128)S(1)}, u32[]{:S(2)}, u32[]{:S(2)}) %collective-permute-start.11) | collective-permute-done | bytes 524320 | tf_op jit(solution)/shard_map/ppermute | solution.py:39
  70.4 1.9 %collective-permute-start.15 = (f32[2,16,4096]{2,1,0:T(8,128)S(1)}, f32[2,16,4096]{2,1,0:T(8,128)S(1)}, u32[]{:S(2)}, u32[]{:S(2)}) collective-permute-start(f32[2,16,4096]{2,1,0:T(8,128)S(1)} %bitcast_add_fusion.2), channel_id=1, source_target_pairs={{0,4},{4,8},{8,12},{12,16},{16,20},{20,24},{24,28},{28,0},{1,5},{5... | collective-permute-start | bytes 1572872 | tf_op jit(solution)/shard_map/ppermute | solution.py:39
  72.4 5.3 %collective-permute-start.16 = (f32[2,16,4096]{2,1,0:T(8,128)S(1)}, f32[2,16,4096]{2,1,0:T(8,128)S(1)}, u32[]{:S(2)}, u32[]{:S(2)}) collective-permute-start(f32[2,16,4096]{2,1,0:T(8,128)S(1)} %bitcast_add_fusion.3), channel_id=1, source_target_pairs={{0,28},{4,0},{8,4},{12,8},{16,12},{20,16},{24,20},{28,24},{1,29},{... | collective-permute-start | bytes 1572872 | tf_op jit(solution)/shard_map/ppermute | solution.py:39
  77.8 3.8 %collective-permute-done.9 = f32[2,16,4096]{2,1,0:T(8,128)S(1)} collective-permute-done((f32[2,16,4096]{2,1,0:T(8,128)S(1)}, f32[2,16,4096]{2,1,0:T(8,128)S(1)}, u32[]{:S(2)}, u32[]{:S(2)}) %collective-permute-start.9) | collective-permute-done | bytes 524320 | tf_op jit(solution)/shard_map/ppermute | solution.py:39
  81.6 2.0 %collective-permute-done.13 = f32[2,16,4096]{2,1,0:T(8,128)S(1)} collective-permute-done((f32[2,16,4096]{2,1,0:T(8,128)S(1)}, f32[2,16,4096]{2,1,0:T(8,128)S(1)}, u32[]{:S(2)}, u32[]{:S(2)}) %collective-permute-start.13) | collective-permute-done | bytes 524320 | tf_op jit(solution)/shard_map/ppermute | solution.py:39
  83.7 17.4 %collective-permute-start.14 = (f32[16,4096]{1,0:T(8,128)S(1)}, f32[16,4096]{1,0:T(8,128)S(1)}, u32[]{:S(2)}, u32[]{:S(2)}) collective-permute-start(f32[16,4096]{1,0:T(8,128)S(1)} %select_bitcast_fusion.1), channel_id=1, source_target_pairs={{0,32},{32,0},{1,33},{33,1},{2,34},{34,2},{3,35},{35,3},{4,36},{36... | collective-permute-start | bytes 786440 | tf_op jit(solution)/shard_map/ppermute | solution.py:39
  101.1 0.1 fusion.3
  101.3 11.1 %collective-permute-start.17 = (f32[16,4096]{1,0:T(8,128)S(1)}, f32[16,4096]{1,0:T(8,128)S(1)}, u32[]{:S(2)}, u32[]{:S(2)}) collective-permute-start(f32[16,4096]{1,0:T(8,128)S(1)} %select_bitcast_fusion), channel_id=1, source_target_pairs={{0,32},{32,0},{1,33},{33,1},{2,34},{34,2},{3,35},{35,3},{4,36},{36... | collective-permute-start | bytes 786440 | tf_op jit(solution)/shard_map/ppermute | solution.py:39
  113.1 13.8 %collective-permute-done.17 = f32[16,4096]{1,0:T(8,128)S(1)} collective-permute-done((f32[16,4096]{1,0:T(8,128)S(1)}, f32[16,4096]{1,0:T(8,128)S(1)}, u32[]{:S(2)}, u32[]{:S(2)}) %collective-permute-start.17) | collective-permute-done | bytes 262176 | tf_op jit(solution)/shard_map/ppermute | solution.py:39
  126.8 0.2 multiply_reduce_fusion.2
  127.0 0.2 multiply_reduce_fusion.3
  127.2 0.6 broadcast_in_dim.16
  127.8 15.9 %all-to-all-start = ((f32[12,1,128]{2,1,0:T(1,128)}), f32[12,1,128]{2,1,0:T(1,128)S(1)}, u32[]{:S(2)}, u32[]{:S(2)}) async-start(f32[12,1,128]{2,1,0:T(1,128)} %broadcast_in_dim.16), calls=%async_computation | async-start | bytes 12288 | tf_op jit(solution)/shard_map/all_to_all | solution.py:16
  143.7 0.1 fusion.5
  143.7 7.8 %all-to-all-done = f32[12,1,128]{2,1,0:T(1,128)S(1)} async-done(((f32[12,1,128]{2,1,0:T(1,128)}), f32[12,1,128]{2,1,0:T(1,128)S(1)}, u32[]{:S(2)}, u32[]{:S(2)}) %all-to-all-start) | async-done | bytes 6176 | tf_op jit(solution)/shard_map/all_to_all | solution.py:16
  151.6 0.1 select_reduce_fusion.1
  151.8 0.1 select_maximum_fusion
  151.8 0.6 broadcast_in_dim.17
  152.5 17.7 %all-to-all-start.1 = ((f32[64,1,128]{2,1,0:T(1,128)}), f32[64,1,128]{2,1,0:T(1,128)S(1)}, u32[]{:S(2)}, u32[]{:S(2)}) async-start(f32[64,1,128]{2,1,0:T(1,128)} %broadcast_in_dim.17), calls=%async_computation.1 | async-start | bytes 65536 | tf_op jit(solution)/shard_map/all_to_all | solution.py:16
  170.2 15.5 %all-to-all-done.1 = f32[64,1,128]{2,1,0:T(1,128)S(1)} async-done(((f32[64,1,128]{2,1,0:T(1,128)}), f32[64,1,128]{2,1,0:T(1,128)S(1)}, u32[]{:S(2)}, u32[]{:S(2)}) %all-to-all-start.1) | async-done | bytes 32800 | tf_op jit(solution)/shard_map/all_to_all | solution.py:16
  185.7 0.1 slice_reduce_fusion
  185.8 0.1 reshape.52
  185.9 0.1 select_reduce_fusion
  186.0 0.6 sub.18
  (45 shorter events, 0.9 us)
Async XLA Ops:
  0.0 1.0 copy-start
  1.0 11.7 %copy-start.5 = (bf16[1,512,8192]{2,1,0:T(8,128)(2,1)S(1)}, bf16[1,512,8192]{2,1,0:T(8,128)(2,1)}, u32[]{:S(2)}) copy-start(bf16[1,512,8192]{2,1,0:T(8,128)(2,1)} %param.7) | copy-start | bytes 25165828
  4.5 8.0 %copy-start.3 = (f32[8,2,16,4096]{3,2,1,0:T(8,128)}, f32[8,2,16,4096]{3,2,1,0:T(8,128)S(1)}, u32[]{:S(2)}) copy-start(f32[8,2,16,4096]{3,2,1,0:T(8,128)S(1)} %fusion.2) | copy-start | bytes 12582916
  4.6 18.0 %collective-permute-start = (f32[16,4096]{1,0:T(8,128)S(1)}, f32[16,4096]{1,0:T(8,128)S(1)}, u32[]{:S(2)}, u32[]{:S(2)}) collective-permute-start(f32[16,4096]{1,0:T(8,128)S(1)} %get-tuple-element.43), channel_id=1, source_target_pairs={{0,4},{4,8},{8,12},{12,16},{16,20},{20,24},{24,28},{28,0},{1,5},{5... | collective-permute-start | bytes 786440 | tf_op jit(solution)/shard_map/ppermute | solution.py:39
  8.8 17.3 %collective-permute-start.4 = (f32[16,4096]{1,0:T(8,128)S(1)}, f32[16,4096]{1,0:T(8,128)S(1)}, u32[]{:S(2)}, u32[]{:S(2)}) collective-permute-start(f32[16,4096]{1,0:T(8,128)S(1)} %get-tuple-element.44), channel_id=1, source_target_pairs={{0,28},{4,0},{8,4},{12,8},{16,12},{20,16},{24,20},{28,24},{1,29},{... | collective-permute-start | bytes 786440 | tf_op jit(solution)/shard_map/ppermute | solution.py:39
  13.9 2.0 %copy-start.1 = (f32[256,4096]{1,0:T(8,128)}, f32[256,4096]{1,0:T(8,128)S(1)}, u32[]{:S(2)}) copy-start(f32[256,4096]{1,0:T(8,128)S(1)} %fusion) | copy-start | bytes 12582916
  15.9 15.8 %collective-permute-start.3 = (f32[16,4096]{1,0:T(8,128)S(1)}, f32[16,4096]{1,0:T(8,128)S(1)}, u32[]{:S(2)}, u32[]{:S(2)}) collective-permute-start(f32[16,4096]{1,0:T(8,128)S(1)} %get-tuple-element.41), channel_id=1, source_target_pairs={{0,4},{4,8},{8,12},{12,16},{16,20},{20,24},{24,28},{28,0},{1,5},{5... | collective-permute-start | bytes 786440 | tf_op jit(solution)/shard_map/ppermute | solution.py:39
  17.9 16.9 %collective-permute-start.2 = (f32[16,4096]{1,0:T(8,128)S(1)}, f32[16,4096]{1,0:T(8,128)S(1)}, u32[]{:S(2)}, u32[]{:S(2)}) collective-permute-start(f32[16,4096]{1,0:T(8,128)S(1)} %get-tuple-element.42), channel_id=1, source_target_pairs={{0,28},{4,0},{8,4},{12,8},{16,12},{20,16},{24,20},{28,24},{1,29},{... | collective-permute-start | bytes 786440 | tf_op jit(solution)/shard_map/ppermute | solution.py:39
  22.6 17.9 %copy-start.4 = (f32[8,2,16,4096]{3,2,1,0:T(8,128)S(1)}, f32[8,2,16,4096]{3,2,1,0:T(8,128)}, u32[]{:S(2)}) copy-start(f32[8,2,16,4096]{3,2,1,0:T(8,128)} %copy-done.3) | copy-start | bytes 12582916
  22.6 25.3 %copy-start.2 = (f32[256,4096]{1,0:T(8,128)S(1)}, f32[256,4096]{1,0:T(8,128)}, u32[]{:S(2)}) copy-start(f32[256,4096]{1,0:T(8,128)} %copy-done.1) | copy-start | bytes 12582916
  23.9 16.6 %collective-permute-start.1 = (f32[2,16,4096]{2,1,0:T(8,128)S(1)}, f32[2,16,4096]{2,1,0:T(8,128)S(1)}, u32[]{:S(2)}, u32[]{:S(2)}) collective-permute-start(f32[2,16,4096]{2,1,0:T(8,128)S(1)} %bitcast_add_fusion.10), channel_id=1, source_target_pairs={{0,4},{4,8},{8,12},{12,16},{16,20},{20,24},{24,28},{28,0},{1,5},{5... | collective-permute-start | bytes 1572872 | tf_op jit(solution)/shard_map/ppermute | solution.py:39
  27.1 15.3 %collective-permute-start.8 = (f32[2,16,4096]{2,1,0:T(8,128)S(1)}, f32[2,16,4096]{2,1,0:T(8,128)S(1)}, u32[]{:S(2)}, u32[]{:S(2)}) collective-permute-start(f32[2,16,4096]{2,1,0:T(8,128)S(1)} %bitcast_add_fusion.7), channel_id=1, source_target_pairs={{0,28},{4,0},{8,4},{12,8},{16,12},{20,16},{24,20},{28,24},{1,29},{... | collective-permute-start | bytes 1572872 | tf_op jit(solution)/shard_map/ppermute | solution.py:39
  32.8 15.1 %collective-permute-start.7 = (f32[2,16,4096]{2,1,0:T(8,128)S(1)}, f32[2,16,4096]{2,1,0:T(8,128)S(1)}, u32[]{:S(2)}, u32[]{:S(2)}) collective-permute-start(f32[2,16,4096]{2,1,0:T(8,128)S(1)} %bitcast_add_fusion.8), channel_id=1, source_target_pairs={{0,4},{4,8},{8,12},{12,16},{16,20},{20,24},{24,28},{28,0},{1,5},{5... | collective-permute-start | bytes 1572872 | tf_op jit(solution)/shard_map/ppermute | solution.py:39
  35.9 14.0 %collective-permute-start.6 = (f32[2,16,4096]{2,1,0:T(8,128)S(1)}, f32[2,16,4096]{2,1,0:T(8,128)S(1)}, u32[]{:S(2)}, u32[]{:S(2)}) collective-permute-start(f32[2,16,4096]{2,1,0:T(8,128)S(1)} %bitcast_add_fusion.9), channel_id=1, source_target_pairs={{0,28},{4,0},{8,4},{12,8},{16,12},{20,16},{24,20},{28,24},{1,29},{... | collective-permute-start | bytes 1572872 | tf_op jit(solution)/shard_map/ppermute | solution.py:39
  40.5 18.6 %collective-permute-start.5 = (f32[2,16,4096]{2,1,0:T(8,128)S(1)}, f32[2,16,4096]{2,1,0:T(8,128)S(1)}, u32[]{:S(2)}, u32[]{:S(2)}) collective-permute-start(f32[2,16,4096]{2,1,0:T(8,128)S(1)} %bitcast_add_fusion.11), channel_id=1, source_target_pairs={{0,4},{4,8},{8,12},{12,16},{16,20},{20,24},{24,28},{28,0},{1,5},{5... | collective-permute-start | bytes 1572872 | tf_op jit(solution)/shard_map/ppermute | solution.py:39
  42.5 18.6 %collective-permute-start.12 = (f32[2,16,4096]{2,1,0:T(8,128)S(1)}, f32[2,16,4096]{2,1,0:T(8,128)S(1)}, u32[]{:S(2)}, u32[]{:S(2)}) collective-permute-start(f32[2,16,4096]{2,1,0:T(8,128)S(1)} %bitcast_add_fusion.4), channel_id=1, source_target_pairs={{0,28},{4,0},{8,4},{12,8},{16,12},{20,16},{24,20},{28,24},{1,29},{... | collective-permute-start | bytes 1572872 | tf_op jit(solution)/shard_map/ppermute | solution.py:39
  48.0 22.4 %collective-permute-start.11 = (f32[2,16,4096]{2,1,0:T(8,128)S(1)}, f32[2,16,4096]{2,1,0:T(8,128)S(1)}, u32[]{:S(2)}, u32[]{:S(2)}) collective-permute-start(f32[2,16,4096]{2,1,0:T(8,128)S(1)} %bitcast_add_fusion.5), channel_id=1, source_target_pairs={{0,4},{4,8},{8,12},{12,16},{16,20},{20,24},{24,28},{28,0},{1,5},{5... | collective-permute-start | bytes 1572872 | tf_op jit(solution)/shard_map/ppermute | solution.py:39
  50.0 22.4 %collective-permute-start.10 = (f32[2,16,4096]{2,1,0:T(8,128)S(1)}, f32[2,16,4096]{2,1,0:T(8,128)S(1)}, u32[]{:S(2)}, u32[]{:S(2)}) collective-permute-start(f32[2,16,4096]{2,1,0:T(8,128)S(1)} %bitcast_add_fusion.6), channel_id=1, source_target_pairs={{0,28},{4,0},{8,4},{12,8},{16,12},{20,16},{24,20},{28,24},{1,29},{... | collective-permute-start | bytes 1572872 | tf_op jit(solution)/shard_map/ppermute | solution.py:39
  59.2 22.4 %collective-permute-start.9 = (f32[2,16,4096]{2,1,0:T(8,128)S(1)}, f32[2,16,4096]{2,1,0:T(8,128)S(1)}, u32[]{:S(2)}, u32[]{:S(2)}) collective-permute-start(f32[2,16,4096]{2,1,0:T(8,128)S(1)} %bitcast_add_fusion.12), channel_id=1, source_target_pairs={{0,4},{4,8},{8,12},{12,16},{16,20},{20,24},{24,28},{28,0},{1,5},{5... | collective-permute-start | bytes 1572872 | tf_op jit(solution)/shard_map/ppermute | solution.py:39
  61.2 51.2 %copy-start.6 = (bf16[1,8192]{1,0:T(2,128)(2,1)S(1)}, bf16[1,8192]{1,0:T(2,128)(2,1)}, u32[]{:S(2)}) copy-start(bf16[1,8192]{1,0:T(2,128)(2,1)} %param.8) | copy-start | bytes 49156
  61.2 22.4 %collective-permute-start.13 = (f32[2,16,4096]{2,1,0:T(8,128)S(1)}, f32[2,16,4096]{2,1,0:T(8,128)S(1)}, u32[]{:S(2)}, u32[]{:S(2)}) collective-permute-start(f32[2,16,4096]{2,1,0:T(8,128)S(1)} %bitcast_add_fusion.1), channel_id=1, source_target_pairs={{0,28},{4,0},{8,4},{12,8},{16,12},{20,16},{24,20},{28,24},{1,29},{... | collective-permute-start | bytes 1572872 | tf_op jit(solution)/shard_map/ppermute | solution.py:39
  70.4 73.3 %copy-start.7 = (s32[256,1]{0,1:T(1,128)S(1)}, s32[256,1]{0,1:T(1,128)}, u32[]{:S(2)}) copy-start(s32[256,1]{0,1:T(1,128)} %param.6) | copy-start | bytes 3076
  70.4 30.7 %collective-permute-start.15 = (f32[2,16,4096]{2,1,0:T(8,128)S(1)}, f32[2,16,4096]{2,1,0:T(8,128)S(1)}, u32[]{:S(2)}, u32[]{:S(2)}) collective-permute-start(f32[2,16,4096]{2,1,0:T(8,128)S(1)} %bitcast_add_fusion.2), channel_id=1, source_target_pairs={{0,4},{4,8},{8,12},{12,16},{16,20},{20,24},{24,28},{28,0},{1,5},{5... | collective-permute-start | bytes 1572872 | tf_op jit(solution)/shard_map/ppermute | solution.py:39
  72.4 28.7 %collective-permute-start.16 = (f32[2,16,4096]{2,1,0:T(8,128)S(1)}, f32[2,16,4096]{2,1,0:T(8,128)S(1)}, u32[]{:S(2)}, u32[]{:S(2)}) collective-permute-start(f32[2,16,4096]{2,1,0:T(8,128)S(1)} %bitcast_add_fusion.3), channel_id=1, source_target_pairs={{0,28},{4,0},{8,4},{12,8},{16,12},{20,16},{24,20},{28,24},{1,29},{... | collective-permute-start | bytes 1572872 | tf_op jit(solution)/shard_map/ppermute | solution.py:39
  83.7 43.3 %collective-permute-start.14 = (f32[16,4096]{1,0:T(8,128)S(1)}, f32[16,4096]{1,0:T(8,128)S(1)}, u32[]{:S(2)}, u32[]{:S(2)}) collective-permute-start(f32[16,4096]{1,0:T(8,128)S(1)} %select_bitcast_fusion.1), channel_id=1, source_target_pairs={{0,32},{32,0},{1,33},{33,1},{2,34},{34,2},{3,35},{35,3},{4,36},{36... | collective-permute-start | bytes 786440 | tf_op jit(solution)/shard_map/ppermute | solution.py:39
  101.3 25.6 %collective-permute-start.17 = (f32[16,4096]{1,0:T(8,128)S(1)}, f32[16,4096]{1,0:T(8,128)S(1)}, u32[]{:S(2)}, u32[]{:S(2)}) collective-permute-start(f32[16,4096]{1,0:T(8,128)S(1)} %select_bitcast_fusion), channel_id=1, source_target_pairs={{0,32},{32,0},{1,33},{33,1},{2,34},{34,2},{3,35},{35,3},{4,36},{36... | collective-permute-start | bytes 786440 | tf_op jit(solution)/shard_map/ppermute | solution.py:39
  127.8 23.8 %all-to-all-start = ((f32[12,1,128]{2,1,0:T(1,128)}), f32[12,1,128]{2,1,0:T(1,128)S(1)}, u32[]{:S(2)}, u32[]{:S(2)}) async-start(f32[12,1,128]{2,1,0:T(1,128)} %broadcast_in_dim.16), calls=%async_computation | async-start | bytes 12288 | tf_op jit(solution)/shard_map/all_to_all | solution.py:16
  152.5 33.2 %all-to-all-start.1 = ((f32[64,1,128]{2,1,0:T(1,128)}), f32[64,1,128]{2,1,0:T(1,128)S(1)}, u32[]{:S(2)}, u32[]{:S(2)}) async-start(f32[64,1,128]{2,1,0:T(1,128)} %broadcast_in_dim.17), calls=%async_computation.1 | async-start | bytes 65536 | tf_op jit(solution)/shard_map/all_to_all | solution.py:16
where the time goes:
time: 187 us
  starting transfers between devices  118 us (63%)
  waiting for transfers between devices  51.5 us (28%)
  other arithmetic  6.65 us (4%)
  matrix products  4.89 us (3%)
  local copies, waits for them, and re-layouts  4.47 us (2%)
    ppermute x18, starting transfers between devices, ship(): return lax.ppermute(value, axis, pairs)  84.4 us
    all_to_all x2, starting transfers between devices, everyone(): return lax.all_to_all(copies, axes, 0, 0, tiled=True)  33.5 us
    ppermute x18, waiting for transfers between devices, ship(): return lax.ppermute(value, axis, pairs)  28.1 us
    all_to_all x2, waiting for transfers between devices, everyone(): return lax.all_to_all(copies, axes, 0, 0, tiled=True)  23.4 us
    add x14, other arithmetic, join(): total = total + value  5.12 us
    dot_general x2, matrix products, body(): jnp.dot(after_last(rows), matrix[:, cuts[g]:cuts[g + 1]], preferred_eleme...  4.89 us
  transfers between devices with their start and end apart: 20, of which 8 were waited for; matrix products, arithmetic and copies ran while one was open for 4% of the time, Pallas kernels for 0%

commit v1 on v0

--- a/solution.py
+++ b/solution.py
@@ -5,7 +5,8 @@
 
 
 ZH = 2
-SPLITS = (4096, 4096)
+SPLITS = (3584, 3328)
+Z_FIRST = 1280
 LANES = 128
 
 
@@ -59,8 +60,17 @@
         opposite = owned_by(g, y + far)
         ups.append(along(opposite[0], 1)[None])
         downs.append(along(opposite[1], -1)[None])
+
+    def z_sides(value):
+        return jnp.where(zh == 0, value[:, 0], value[:, 1]), jnp.where(zh == 0, value[:, 1], value[:, 0])
+
     for step in range(far - 1, 0, -1):
         for g in spans:
+            if step == far - 1 and g == 1:
+                product = jnp.dot(after_last(rows), matrix[:, cuts[-1] :], preferred_element_type=jnp.float32)
+                kept, given = z_sides(product.reshape(ring, ZH, own, Z_FIRST))
+                received = ship(given, "zh", swap)
+                z_summed = kept + received
             up = after_last(ups[g])
             if step == far - 1:
                 up = lax.pad(up, 0.0, ((0, 1, 0), (0, 0, 0), (0, 0, 0)))
@@ -72,26 +82,37 @@
 
     gain = head[0].astype(jnp.float32)
     squares, numer = 0.0, 0.0
+
+    def measured(full, first, last):
+        return jnp.sum(full * full, axis=1), jnp.sum(full * gain[None, first:last], axis=1)
+
+    done = []
     for g in spans:
         total = join(owned_by(g, y), after_last(ups[g]), downs[g])
         kept = jnp.where(zh == 0, total[0], total[1])
         given = jnp.where(zh == 0, total[1], total[0])
-        full = kept + ship(given, "zh", swap)
-        squares = squares + jnp.sum(full * full, axis=1)
-        numer = numer + jnp.sum(full * gain[None, cuts[g] : cuts[g + 1]], axis=1)
+        done.append((kept + ship(given, "zh", swap), cuts[g], cuts[g + 1]))
+        if g == 0:
+            sent.append(given)
+            turned = lax.all_to_all(z_summed, "y", 0, 0, tiled=True)
+    done.append((jnp.sum(turned, axis=0), cuts[-1], width))
+    for full, first, last in done:
+        square, product = measured(full, first, last)
+        squares, numer = squares + square, numer + product
     score = coef[0] * numer * lax.rsqrt(squares / width + 1e-05)
 
     names = jnp.arange(groups, dtype=jnp.int32)[None, :]
     target = dest[:, 0]
-    own_target = lax.dynamic_slice_in_dim(target, (y * ZH + zh) * own, own)
-    own_member = (own_target[:, None] == names).astype(jnp.float32)
-    combined = jnp.sum(everyone(score, "section"), axis=0)[:own]
-    totals = jnp.sum(own_member * combined[:, None], axis=0)
-    counts = jnp.sum(own_member, axis=0)
-    pieces = everyone(jnp.concatenate([combined, totals, counts]), ("dp", "y", "zh"))
-    pieces = pieces.reshape(groups, ring * ZH, LANES)
-    mine = lax.dynamic_index_in_dim(pieces, lax.axis_index("dp"), 0, False)[:, :own].reshape(tokens)
-    tail = jnp.sum(pieces[:, :, own : own + 2 * groups], axis=(0, 1))
+    pair = ZH * own
+    pair_target = lax.dynamic_slice_in_dim(target, y * pair, pair)
+    pair_member = (pair_target[:, None] == names).astype(jnp.float32)
+    scores = everyone(score, ("zh", "section")).reshape(ZH, -1, LANES)
+    combined = jnp.sum(scores, axis=1)[:, :own].reshape(pair)
+    totals = jnp.sum(pair_member * combined[:, None], axis=0)
+    counts = jnp.sum(pair_member, axis=0)
+    pieces = everyone(jnp.concatenate([combined, totals, counts]), ("dp", "y")).reshape(groups, ring, LANES)
+    mine = lax.dynamic_index_in_dim(pieces, lax.axis_index("dp"), 0, False)[:, :pair].reshape(tokens)
+    tail = jnp.sum(pieces[:, :, pair : pair + 2 * groups], axis=(0, 1))
     group_mean = tail[:groups] / tail[groups:]
     member = (target[:, None] == names).astype(jnp.float32)
     return mine - jnp.sum(member * group_mean[None, :], axis=1)

time: 187 us -> 205 us (1.096)
  starting transfers between devices: 118 us -> 136 us
  waiting for transfers between devices: 51.5 us -> 38.6 us
  other arithmetic: 6.65 us -> 15.4 us
  matrix products: 4.89 us -> 7.98 us
    all_to_all x2, starting transfers between devices: 33.5 us -> 49.5 us  [everyone(): return lax.all_to_all(copies, axes, 0, 0, tiled=True)]
    ppermute x18 -> x19, waiting for transfers between devices: 28.1 us -> 20.6 us  [ship(): return lax.ppermute(value, axis, pairs)]
    add x14, other arithmetic: 5.12 us -> 12 us  [join(): total = total + value]
    all_to_all x0 -> x1, starting transfers between devices: none -> 6.3 us  [body(): turned = lax.all_to_all(z_summed, 'y', 0, 0, tiled=True)]
    all_to_all x2, waiting for transfers between devices: 23.4 us -> 18 us  [everyone(): return lax.all_to_all(copies, axes, 0, 0, tiled=True)]
    ppermute x18 -> x19, starting transfers between devices: 84.4 us -> 79.7 us  [ship(): return lax.ppermute(value, axis, pairs)]
  transfers between devices with their start and end apart: 20 -> 22, of which waited for: 8 -> 8; matrix products, arithmetic and copies ran while one was open for 4% -> 9% of each run, Pallas kernels for 0% -> 0%
where the time goes in v1:
time: 205 us; the launch traced here: 204 us
  starting transfers between devices  136 us (66%)
  waiting for transfers between devices  38.6 us (19%)
  other arithmetic  15.4 us (8%)
  matrix products  7.98 us (4%)
  local copies, waits for them, and re-layouts  4.88 us (2%)
    ppermute x19, starting transfers between devices, ship(): return lax.ppermute(value, axis, pairs)  79.7 us
    all_to_all x2, starting transfers between devices, everyone(): return lax.all_to_all(copies, axes, 0, 0, tiled=True)  49.5 us
    ppermute x19, waiting for transfers between devices, ship(): return lax.ppermute(value, axis, pairs)  20.6 us
    all_to_all x2, waiting for transfers between devices, everyone(): return lax.all_to_all(copies, axes, 0, 0, tiled=True)  18 us
    add x14, other arithmetic, join(): total = total + value  12 us
    all_to_all x1, starting transfers between devices, body(): turned = lax.all_to_all(z_summed, 'y', 0, 0, tiled=True)  6.3 us
    dot_general x2, matrix products, body(): jnp.dot(after_last(rows), matrix[:, cuts[g]:cuts[g + 1]], preferred_eleme...  6.16 us
  transfers between devices with their start and end apart: 22, of which 8 were waited for; matrix products, arithmetic and copies ran while one was open for 9% of the time, Pallas kernels for 0%

profile of v1, /device:TPU:1, one launch (start us, length us, event | category | flops | bytes accessed | tf_op | source)
XLA Modules:
  0.0 203.7 jit_solution(4381713884008469688)
XLA Ops:
  0.0 0.9 copy-done
  1.0 3.1 %fusion = f32[8,2,16,3584]{3,2,1,0:T(8,128)S(1)} fusion(bf16[8,2,16,512]{3,2,1,0:T(8,128)(2,1)S(1)} %bitcast.92, bf16[512,8192]{1,0:T(8,128)(2,1)} %bitcast.103), kind=kOutput, calls=%fused_computation.1 | convolution fusion | flops 939524096 | bytes 7602176 | tf_op jit(solution)/shard_map/dot_general | solution.py:58
  4.2 4.0 %collective-permute-start = (f32[16,3584]{1,0:T(8,128)S(1)}, f32[16,3584]{1,0:T(8,128)S(1)}, u32[]{:S(2)}, u32[]{:S(2)}) collective-permute-start(f32[16,3584]{1,0:T(8,128)S(1)} %get-tuple-element.45), channel_id=1, source_target_pairs={{0,4},{4,8},{8,12},{12,16},{16,20},{20,24},{24,28},{28,0},{1,5},{5... | collective-permute-start | bytes 688136 | tf_op jit(solution)/shard_map/ppermute | solution.py:40
  8.2 3.8 %collective-permute-start.4 = (f32[16,3584]{1,0:T(8,128)S(1)}, f32[16,3584]{1,0:T(8,128)S(1)}, u32[]{:S(2)}, u32[]{:S(2)}) collective-permute-start(f32[16,3584]{1,0:T(8,128)S(1)} %get-tuple-element.46), channel_id=1, source_target_pairs={{0,28},{4,0},{8,4},{12,8},{16,12},{20,16},{24,20},{28,24},{1,29},{... | collective-permute-start | bytes 688136 | tf_op jit(solution)/shard_map/ppermute | solution.py:40
  12.0 3.0 %fusion.1 = f32[256,3328]{1,0:T(8,128)S(1)} fusion(bf16[256,512]{1,0:T(8,128)(2,1)S(1)} %bitcast.90, bf16[512,8192]{1,0:T(8,128)(2,1)} %bitcast.104), kind=kOutput, calls=%fused_computation.2 | convolution fusion | flops 872415232 | bytes 7077888 | tf_op jit(solution)/shard_map/dot_general | solution.py:58
  15.1 1.7 copy-done.1
  16.9 1.9 collective-permute-start.3
  18.8 4.6 %collective-permute-start.2 = (f32[16,3328]{1,0:T(8,128)S(1)}, f32[16,3328]{1,0:T(8,128)S(1)}, u32[]{:S(2)}, u32[]{:S(2)}) collective-permute-start(f32[16,3328]{1,0:T(8,128)S(1)} %get-tuple-element.48), channel_id=1, source_target_pairs={{0,28},{4,0},{8,4},{12,8},{16,12},{20,16},{24,20},{28,24},{1,29},{... | collective-permute-start | bytes 638984 | tf_op jit(solution)/shard_map/ppermute | solution.py:40
  24.3 1.2 bitcast_add_fusion.4
  25.5 1.9 collective-permute-start.1
  27.4 1.1 bitcast_add_fusion.3
  28.5 4.6 %collective-permute-start.8 = (f32[2,16,3584]{2,1,0:T(8,128)S(1)}, f32[2,16,3584]{2,1,0:T(8,128)S(1)}, u32[]{:S(2)}, u32[]{:S(2)}) collective-permute-start(f32[2,16,3584]{2,1,0:T(8,128)S(1)} %bitcast_add_fusion.3), channel_id=1, source_target_pairs={{0,28},{4,0},{8,4},{12,8},{16,12},{20,16},{24,20},{28,24},{1,29},{... | collective-permute-start | bytes 1376264 | tf_op jit(solution)/shard_map/ppermute | solution.py:40
  33.1 1.8 fusion.3
  35.0 14.9 %collective-permute-start.18 = (f32[8,16,1280]{2,1,0:T(8,128)S(1)}, f32[8,16,1280]{2,1,0:T(8,128)S(1)}, u32[]{:S(2)}, u32[]{:S(2)}) collective-permute-start(f32[8,16,1280]{2,1,0:T(8,128)S(1)} %fusion.5), channel_id=1, source_target_pairs={{0,32},{32,0},{1,33},{33,1},{2,34},{34,2},{3,35},{35,3},{4,36},{36... | collective-permute-start | bytes 1966088 | tf_op jit(solution)/shard_map/ppermute | solution.py:40
  49.9 1.9 collective-permute-start.7
  51.9 4.6 %collective-permute-start.6 = (f32[2,16,3328]{2,1,0:T(8,128)S(1)}, f32[2,16,3328]{2,1,0:T(8,128)S(1)}, u32[]{:S(2)}, u32[]{:S(2)}) collective-permute-start(f32[2,16,3328]{2,1,0:T(8,128)S(1)} %bitcast_add_fusion.14), channel_id=1, source_target_pairs={{0,28},{4,0},{8,4},{12,8},{16,12},{20,16},{24,20},{28,24},{1,29},{... | collective-permute-start | bytes 1277960 | tf_op jit(solution)/shard_map/ppermute | solution.py:40
  56.5 1.1 bitcast_add_fusion.5
  57.6 1.9 collective-permute-start.5
  59.5 1.1 bitcast_add_fusion.2
  60.6 4.6 %collective-permute-start.12 = (f32[2,16,3584]{2,1,0:T(8,128)S(1)}, f32[2,16,3584]{2,1,0:T(8,128)S(1)}, u32[]{:S(2)}, u32[]{:S(2)}) collective-permute-start(f32[2,16,3584]{2,1,0:T(8,128)S(1)} %bitcast_add_fusion.2), channel_id=1, source_target_pairs={{0,28},{4,0},{8,4},{12,8},{16,12},{20,16},{24,20},{28,24},{1,29},{... | collective-permute-start | bytes 1376264 | tf_op jit(solution)/shard_map/ppermute | solution.py:40
  65.3 1.9 collective-permute-start.11
  67.2 0.8 bitcast_add_fusion.12
  68.0 4.6 %collective-permute-start.10 = (f32[2,16,3328]{2,1,0:T(8,128)}, f32[2,16,3328]{2,1,0:T(8,128)}, u32[]{:S(2)}, u32[]{:S(2)}) collective-permute-start(f32[2,16,3328]{2,1,0:T(8,128)} %bitcast_add_fusion.12), channel_id=1, source_target_pairs={{0,28},{4,0},{8,4},{12,8},{16,12},{20,16},{24,20},{28,24},{1,29},{... | collective-permute-start | bytes 1277960 | tf_op jit(solution)/shard_map/ppermute | solution.py:40
  72.6 0.9 bitcast_add_fusion
  73.5 6.3 %all-to-all-start = ((f32[8,16,1280]{2,1,0:T(8,128)}), f32[8,16,1280]{2,1,0:T(8,128)S(1)}, u32[]{:S(2)}, u32[]{:S(2)}) async-start(f32[8,16,1280]{2,1,0:T(8,128)} %bitcast_add_fusion), calls=%async_computation | async-start | bytes 1310720 | tf_op jit(solution)/shard_map/all_to_all | solution.py:97
  79.8 1.1 bitcast_add_fusion.6
  80.9 3.4 %collective-permute-start.9 = (f32[2,16,3584]{2,1,0:T(8,128)S(1)}, f32[2,16,3584]{2,1,0:T(8,128)S(1)}, u32[]{:S(2)}, u32[]{:S(2)}) collective-permute-start(f32[2,16,3584]{2,1,0:T(8,128)S(1)} %bitcast_add_fusion.6), channel_id=1, source_target_pairs={{0,4},{4,8},{8,12},{12,16},{16,20},{20,24},{24,28},{28,0},{1,5},{5... | collective-permute-start | bytes 1376264 | tf_op jit(solution)/shard_map/ppermute | solution.py:40
  84.3 1.1 bitcast_add_fusion.1
  85.3 3.1 %collective-permute-start.13 = (f32[2,16,3584]{2,1,0:T(8,128)S(1)}, f32[2,16,3584]{2,1,0:T(8,128)S(1)}, u32[]{:S(2)}, u32[]{:S(2)}) collective-permute-start(f32[2,16,3584]{2,1,0:T(8,128)S(1)} %bitcast_add_fusion.1), channel_id=1, source_target_pairs={{0,28},{4,0},{8,4},{12,8},{16,12},{20,16},{24,20},{28,24},{1,29},{... | collective-permute-start | bytes 1376264 | tf_op jit(solution)/shard_map/ppermute | solution.py:40
  88.5 1.2 bitcast_add_fusion.9
  89.7 2.1 %collective-permute-start.15 = (f32[2,16,3328]{2,1,0:T(8,128)S(1)}, f32[2,16,3328]{2,1,0:T(8,128)S(1)}, u32[]{:S(2)}, u32[]{:S(2)}) collective-permute-start(f32[2,16,3328]{2,1,0:T(8,128)S(1)} %bitcast_add_fusion.9), channel_id=1, source_target_pairs={{0,4},{4,8},{8,12},{12,16},{16,20},{20,24},{24,28},{28,0},{1,5},{5... | collective-permute-start | bytes 1277960 | tf_op jit(solution)/shard_map/ppermute | solution.py:40
  91.8 1.2 bitcast_add_fusion.10
  93.1 4.3 %collective-permute-start.16 = (f32[2,16,3328]{2,1,0:T(8,128)S(1)}, f32[2,16,3328]{2,1,0:T(8,128)S(1)}, u32[]{:S(2)}, u32[]{:S(2)}) collective-permute-start(f32[2,16,3328]{2,1,0:T(8,128)S(1)} %bitcast_add_fusion.10), channel_id=1, source_target_pairs={{0,28},{4,0},{8,4},{12,8},{16,12},{20,16},{24,20},{28,24},{1,29},{... | collective-permute-start | bytes 1277960 | tf_op jit(solution)/shard_map/ppermute | solution.py:40
  97.4 8.0 %collective-permute-done.9 = f32[2,16,3584]{2,1,0:T(8,128)S(1)} collective-permute-done((f32[2,16,3584]{2,1,0:T(8,128)S(1)}, f32[2,16,3584]{2,1,0:T(8,128)S(1)}, u32[]{:S(2)}, u32[]{:S(2)}) %collective-permute-start.9) | collective-permute-done | bytes 458784 | tf_op jit(solution)/shard_map/ppermute | solution.py:40
  105.4 1.1 collective-permute-done.13
  106.5 1.1 fusion.6
  107.6 6.9 %collective-permute-done.15 = f32[2,16,3328]{2,1,0:T(8,128)S(1)} collective-permute-done((f32[2,16,3328]{2,1,0:T(8,128)S(1)}, f32[2,16,3328]{2,1,0:T(8,128)S(1)}, u32[]{:S(2)}, u32[]{:S(2)}) %collective-permute-start.15) | collective-permute-done | bytes 426016 | tf_op jit(solution)/shard_map/ppermute | solution.py:40
  114.5 1.1 collective-permute-done.16
  115.6 1.1 fusion.7
  116.7 1.9 collective-permute-start.17
  118.7 9.7 %collective-permute-start.14 = (f32[16,3584]{1,0:T(8,128)S(1)}, f32[16,3584]{1,0:T(8,128)S(1)}, u32[]{:S(2)}, u32[]{:S(2)}) collective-permute-start(f32[16,3584]{1,0:T(8,128)S(1)} %select_bitcast_fusion), channel_id=1, source_target_pairs={{0,32},{32,0},{1,33},{33,1},{2,34},{34,2},{3,35},{35,3},{4,36},{36... | collective-permute-start | bytes 688136 | tf_op jit(solution)/shard_map/ppermute | solution.py:40
  128.4 1.2 collective-permute-done.17
  129.8 2.3 %collective-permute-done.14 = f32[16,3584]{1,0:T(8,128)S(1)} collective-permute-done((f32[16,3584]{1,0:T(8,128)S(1)}, f32[16,3584]{1,0:T(8,128)S(1)}, u32[]{:S(2)}, u32[]{:S(2)}) %collective-permute-start.14) | collective-permute-done | bytes 229408 | tf_op jit(solution)/shard_map/ppermute | solution.py:40
  133.1 40.2 %all-to-all-start.1 = ((f32[24,1,128]{2,1,0:T(1,128)}), f32[24,1,128]{2,1,0:T(1,128)S(1)}, u32[]{:S(2)}, u32[]{:S(2)}) async-start(f32[24,1,128]{2,1,0:T(1,128)} %broadcast_in_dim.16), calls=%async_computation.1 | async-start | bytes 24576 | tf_op jit(solution)/shard_map/all_to_all | solution.py:17
  173.3 9.3 %all-to-all-done.1 = f32[24,1,128]{2,1,0:T(1,128)S(1)} async-done(((f32[24,1,128]{2,1,0:T(1,128)}), f32[24,1,128]{2,1,0:T(1,128)S(1)}, u32[]{:S(2)}, u32[]{:S(2)}) %all-to-all-start.1) | async-done | bytes 12320 | tf_op jit(solution)/shard_map/all_to_all | solution.py:17
  183.2 0.7 reduce.9
  184.8 9.3 %all-to-all-start.2 = ((f32[32,1,128]{2,1,0:T(1,128)}), f32[32,1,128]{2,1,0:T(1,128)S(1)}, u32[]{:S(2)}, u32[]{:S(2)}) async-start(f32[32,1,128]{2,1,0:T(1,128)} %broadcast_in_dim.17), calls=%async_computation.2 | async-start | bytes 32768 | tf_op jit(solution)/shard_map/all_to_all | solution.py:17
  194.2 8.7 %all-to-all-done.2 = f32[32,1,128]{2,1,0:T(1,128)S(1)} async-done(((f32[32,1,128]{2,1,0:T(1,128)}), f32[32,1,128]{2,1,0:T(1,128)S(1)}, u32[]{:S(2)}, u32[]{:S(2)}) %all-to-all-start.2) | async-done | bytes 16416 | tf_op jit(solution)/shard_map/all_to_all | solution.py:17
  (57 shorter events, 4.1 us)
Async XLA Ops:
  0.0 1.0 copy-start
  4.1 7.9 %copy-start.3 = (f32[8,2,16,3584]{3,2,1,0:T(8,128)}, f32[8,2,16,3584]{3,2,1,0:T(8,128)S(1)}, u32[]{:S(2)}) copy-start(f32[8,2,16,3584]{3,2,1,0:T(8,128)S(1)} %fusion) | copy-start | bytes 11010052
  4.2 20.1 %collective-permute-start = (f32[16,3584]{1,0:T(8,128)S(1)}, f32[16,3584]{1,0:T(8,128)S(1)}, u32[]{:S(2)}, u32[]{:S(2)}) collective-permute-start(f32[16,3584]{1,0:T(8,128)S(1)} %get-tuple-element.45), channel_id=1, source_target_pairs={{0,4},{4,8},{8,12},{12,16},{16,20},{20,24},{24,28},{28,0},{1,5},{5... | collective-permute-start | bytes 688136 | tf_op jit(solution)/shard_map/ppermute | solution.py:40
  8.2 19.2 %collective-permute-start.4 = (f32[16,3584]{1,0:T(8,128)S(1)}, f32[16,3584]{1,0:T(8,128)S(1)}, u32[]{:S(2)}, u32[]{:S(2)}) collective-permute-start(f32[16,3584]{1,0:T(8,128)S(1)} %get-tuple-element.46), channel_id=1, source_target_pairs={{0,28},{4,0},{8,4},{12,8},{16,12},{20,16},{24,20},{28,24},{1,29},{... | collective-permute-start | bytes 688136 | tf_op jit(solution)/shard_map/ppermute | solution.py:40
  12.0 11.5 %copy-start.4 = (bf16[1,8192]{1,0:T(2,128)(2,1)S(1)}, bf16[1,8192]{1,0:T(2,128)(2,1)}, u32[]{:S(2)}) copy-start(bf16[1,8192]{1,0:T(2,128)(2,1)} %param.8) | copy-start | bytes 49156
  15.1 1.8 copy-start.1
  16.9 33.0 %collective-permute-start.3 = (f32[16,3328]{1,0:T(8,128)S(1)}, f32[16,3328]{1,0:T(8,128)S(1)}, u32[]{:S(2)}, u32[]{:S(2)}) collective-permute-start(f32[16,3328]{1,0:T(8,128)S(1)} %get-tuple-element.47), channel_id=1, source_target_pairs={{0,4},{4,8},{8,12},{12,16},{16,20},{20,24},{24,28},{28,0},{1,5},{5... | collective-permute-start | bytes 638984 | tf_op jit(solution)/shard_map/ppermute | solution.py:40
  18.8 33.1 %collective-permute-start.2 = (f32[16,3328]{1,0:T(8,128)S(1)}, f32[16,3328]{1,0:T(8,128)S(1)}, u32[]{:S(2)}, u32[]{:S(2)}) collective-permute-start(f32[16,3328]{1,0:T(8,128)S(1)} %get-tuple-element.48), channel_id=1, source_target_pairs={{0,28},{4,0},{8,4},{12,8},{16,12},{20,16},{24,20},{28,24},{1,29},{... | collective-permute-start | bytes 638984 | tf_op jit(solution)/shard_map/ppermute | solution.py:40
  24.2 25.7 %copy-start.2 = (f32[256,3328]{1,0:T(8,128)S(1)}, f32[256,3328]{1,0:T(8,128)}, u32[]{:S(2)}) copy-start(f32[256,3328]{1,0:T(8,128)} %copy-done.1) | copy-start | bytes 10223620
  25.5 31.0 %collective-permute-start.1 = (f32[2,16,3584]{2,1,0:T(8,128)S(1)}, f32[2,16,3584]{2,1,0:T(8,128)S(1)}, u32[]{:S(2)}, u32[]{:S(2)}) collective-permute-start(f32[2,16,3584]{2,1,0:T(8,128)S(1)} %bitcast_add_fusion.4), channel_id=1, source_target_pairs={{0,4},{4,8},{8,12},{12,16},{16,20},{20,24},{24,28},{28,0},{1,5},{5... | collective-permute-start | bytes 1376264 | tf_op jit(solution)/shard_map/ppermute | solution.py:40
  28.5 31.0 %collective-permute-start.8 = (f32[2,16,3584]{2,1,0:T(8,128)S(1)}, f32[2,16,3584]{2,1,0:T(8,128)S(1)}, u32[]{:S(2)}, u32[]{:S(2)}) collective-permute-start(f32[2,16,3584]{2,1,0:T(8,128)S(1)} %bitcast_add_fusion.3), channel_id=1, source_target_pairs={{0,28},{4,0},{8,4},{12,8},{16,12},{20,16},{24,20},{28,24},{1,29},{... | collective-permute-start | bytes 1376264 | tf_op jit(solution)/shard_map/ppermute | solution.py:40
  35.0 37.6 %collective-permute-start.18 = (f32[8,16,1280]{2,1,0:T(8,128)S(1)}, f32[8,16,1280]{2,1,0:T(8,128)S(1)}, u32[]{:S(2)}, u32[]{:S(2)}) collective-permute-start(f32[8,16,1280]{2,1,0:T(8,128)S(1)} %fusion.5), channel_id=1, source_target_pairs={{0,32},{32,0},{1,33},{33,1},{2,34},{34,2},{3,35},{35,3},{4,36},{36... | collective-permute-start | bytes 1966088 | tf_op jit(solution)/shard_map/ppermute | solution.py:40
  49.9 15.3 %collective-permute-start.7 = (f32[2,16,3328]{2,1,0:T(8,128)S(1)}, f32[2,16,3328]{2,1,0:T(8,128)S(1)}, u32[]{:S(2)}, u32[]{:S(2)}) collective-permute-start(f32[2,16,3328]{2,1,0:T(8,128)S(1)} %bitcast_add_fusion.13), channel_id=1, source_target_pairs={{0,4},{4,8},{8,12},{12,16},{16,20},{20,24},{24,28},{28,0},{1,5},{5... | collective-permute-start | bytes 1277960 | tf_op jit(solution)/shard_map/ppermute | solution.py:40
  51.9 15.3 %collective-permute-start.6 = (f32[2,16,3328]{2,1,0:T(8,128)S(1)}, f32[2,16,3328]{2,1,0:T(8,128)S(1)}, u32[]{:S(2)}, u32[]{:S(2)}) collective-permute-start(f32[2,16,3328]{2,1,0:T(8,128)S(1)} %bitcast_add_fusion.14), channel_id=1, source_target_pairs={{0,28},{4,0},{8,4},{12,8},{16,12},{20,16},{24,20},{28,24},{1,29},{... | collective-permute-start | bytes 1277960 | tf_op jit(solution)/shard_map/ppermute | solution.py:40
  57.6 22.2 %collective-permute-start.5 = (f32[2,16,3584]{2,1,0:T(8,128)S(1)}, f32[2,16,3584]{2,1,0:T(8,128)S(1)}, u32[]{:S(2)}, u32[]{:S(2)}) collective-permute-start(f32[2,16,3584]{2,1,0:T(8,128)S(1)} %bitcast_add_fusion.5), channel_id=1, source_target_pairs={{0,4},{4,8},{8,12},{12,16},{16,20},{20,24},{24,28},{28,0},{1,5},{5... | collective-permute-start | bytes 1376264 | tf_op jit(solution)/shard_map/ppermute | solution.py:40
  60.6 23.6 %collective-permute-start.12 = (f32[2,16,3584]{2,1,0:T(8,128)S(1)}, f32[2,16,3584]{2,1,0:T(8,128)S(1)}, u32[]{:S(2)}, u32[]{:S(2)}) collective-permute-start(f32[2,16,3584]{2,1,0:T(8,128)S(1)} %bitcast_add_fusion.2), channel_id=1, source_target_pairs={{0,28},{4,0},{8,4},{12,8},{16,12},{20,16},{24,20},{28,24},{1,29},{... | collective-permute-start | bytes 1376264 | tf_op jit(solution)/shard_map/ppermute | solution.py:40
  65.3 23.2 %collective-permute-start.11 = (f32[2,16,3328]{2,1,0:T(8,128)S(1)}, f32[2,16,3328]{2,1,0:T(8,128)}, u32[]{:S(2)}, u32[]{:S(2)}) collective-permute-start(f32[2,16,3328]{2,1,0:T(8,128)S(1)} %bitcast_add_fusion.11), channel_id=1, source_target_pairs={{0,4},{4,8},{8,12},{12,16},{16,20},{20,24},{24,28},{28,0},{1,5},{5... | collective-permute-start | bytes 1277960 | tf_op jit(solution)/shard_map/ppermute | solution.py:40
  68.0 23.8 %collective-permute-start.10 = (f32[2,16,3328]{2,1,0:T(8,128)}, f32[2,16,3328]{2,1,0:T(8,128)}, u32[]{:S(2)}, u32[]{:S(2)}) collective-permute-start(f32[2,16,3328]{2,1,0:T(8,128)} %bitcast_add_fusion.12), channel_id=1, source_target_pairs={{0,28},{4,0},{8,4},{12,8},{16,12},{20,16},{24,20},{28,24},{1,29},{... | collective-permute-start | bytes 1277960 | tf_op jit(solution)/shard_map/ppermute | solution.py:40
  73.5 58.8 %all-to-all-start = ((f32[8,16,1280]{2,1,0:T(8,128)}), f32[8,16,1280]{2,1,0:T(8,128)S(1)}, u32[]{:S(2)}, u32[]{:S(2)}) async-start(f32[8,16,1280]{2,1,0:T(8,128)} %bitcast_add_fusion), calls=%async_computation | async-start | bytes 1310720 | tf_op jit(solution)/shard_map/all_to_all | solution.py:97
  80.9 24.5 %collective-permute-start.9 = (f32[2,16,3584]{2,1,0:T(8,128)S(1)}, f32[2,16,3584]{2,1,0:T(8,128)S(1)}, u32[]{:S(2)}, u32[]{:S(2)}) collective-permute-start(f32[2,16,3584]{2,1,0:T(8,128)S(1)} %bitcast_add_fusion.6), channel_id=1, source_target_pairs={{0,4},{4,8},{8,12},{12,16},{16,20},{20,24},{24,28},{28,0},{1,5},{5... | collective-permute-start | bytes 1376264 | tf_op jit(solution)/shard_map/ppermute | solution.py:40
  85.3 21.1 %collective-permute-start.13 = (f32[2,16,3584]{2,1,0:T(8,128)S(1)}, f32[2,16,3584]{2,1,0:T(8,128)S(1)}, u32[]{:S(2)}, u32[]{:S(2)}) collective-permute-start(f32[2,16,3584]{2,1,0:T(8,128)S(1)} %bitcast_add_fusion.1), channel_id=1, source_target_pairs={{0,28},{4,0},{8,4},{12,8},{16,12},{20,16},{24,20},{28,24},{1,29},{... | collective-permute-start | bytes 1376264 | tf_op jit(solution)/shard_map/ppermute | solution.py:40
  89.7 24.8 %collective-permute-start.15 = (f32[2,16,3328]{2,1,0:T(8,128)S(1)}, f32[2,16,3328]{2,1,0:T(8,128)S(1)}, u32[]{:S(2)}, u32[]{:S(2)}) collective-permute-start(f32[2,16,3328]{2,1,0:T(8,128)S(1)} %bitcast_add_fusion.9), channel_id=1, source_target_pairs={{0,4},{4,8},{8,12},{12,16},{16,20},{20,24},{24,28},{28,0},{1,5},{5... | collective-permute-start | bytes 1277960 | tf_op jit(solution)/shard_map/ppermute | solution.py:40
  93.0 80.2 %copy-start.5 = (s32[256,1]{0,1:T(1,128)S(1)}, s32[256,1]{0,1:T(1,128)}, u32[]{:S(2)}) copy-start(s32[256,1]{0,1:T(1,128)} %param.6) | copy-start | bytes 3076
  93.1 22.6 %collective-permute-start.16 = (f32[2,16,3328]{2,1,0:T(8,128)S(1)}, f32[2,16,3328]{2,1,0:T(8,128)S(1)}, u32[]{:S(2)}, u32[]{:S(2)}) collective-permute-start(f32[2,16,3328]{2,1,0:T(8,128)S(1)} %bitcast_add_fusion.10), channel_id=1, source_target_pairs={{0,28},{4,0},{8,4},{12,8},{16,12},{20,16},{24,20},{28,24},{1,29},{... | collective-permute-start | bytes 1277960 | tf_op jit(solution)/shard_map/ppermute | solution.py:40
  116.7 12.9 %collective-permute-start.17 = (f32[16,3328]{1,0:T(8,128)S(1)}, f32[16,3328]{1,0:T(8,128)S(1)}, u32[]{:S(2)}, u32[]{:S(2)}) collective-permute-start(f32[16,3328]{1,0:T(8,128)S(1)} %select_bitcast_fusion.1), channel_id=1, source_target_pairs={{0,32},{32,0},{1,33},{33,1},{2,34},{34,2},{3,35},{35,3},{4,36},{36... | collective-permute-start | bytes 638984 | tf_op jit(solution)/shard_map/ppermute | solution.py:40
  118.7 13.4 %collective-permute-start.14 = (f32[16,3584]{1,0:T(8,128)S(1)}, f32[16,3584]{1,0:T(8,128)S(1)}, u32[]{:S(2)}, u32[]{:S(2)}) collective-permute-start(f32[16,3584]{1,0:T(8,128)S(1)} %select_bitcast_fusion), channel_id=1, source_target_pairs={{0,32},{32,0},{1,33},{33,1},{2,34},{34,2},{3,35},{35,3},{4,36},{36... | collective-permute-start | bytes 688136 | tf_op jit(solution)/shard_map/ppermute | solution.py:40
  133.1 49.6 %all-to-all-start.1 = ((f32[24,1,128]{2,1,0:T(1,128)}), f32[24,1,128]{2,1,0:T(1,128)S(1)}, u32[]{:S(2)}, u32[]{:S(2)}) async-start(f32[24,1,128]{2,1,0:T(1,128)} %broadcast_in_dim.16), calls=%async_computation.1 | async-start | bytes 24576 | tf_op jit(solution)/shard_map/all_to_all | solution.py:17
  184.8 18.0 %all-to-all-start.2 = ((f32[32,1,128]{2,1,0:T(1,128)}), f32[32,1,128]{2,1,0:T(1,128)S(1)}, u32[]{:S(2)}, u32[]{:S(2)}) async-start(f32[32,1,128]{2,1,0:T(1,128)} %broadcast_in_dim.17), calls=%async_computation.2 | async-start | bytes 32768 | tf_op jit(solution)/shard_map/all_to_all | solution.py:17

commit v2 on v1

--- a/solution.py
+++ b/solution.py
@@ -1,12 +1,15 @@
 import jax
 import jax.numpy as jnp
 from jax import lax
+from jax.experimental import pallas as pl
+from jax.experimental.pallas import tpu as pltpu
 from jax.sharding import Mesh, PartitionSpec as P
 
 
 ZH = 2
-SPLITS = (3584, 3328)
-Z_FIRST = 1280
+SPLITS = (3584, 3072)
+Z_FIRST = 1536
+BLOCK = 512
 LANES = 128
 
 
@@ -17,10 +20,67 @@
     return lax.all_to_all(copies, axes, 0, 0, tiled=True)
 
 
+def products(rows, weights, place, ring, own):
+    tokens, depth = rows.shape
+    counts = [columns // BLOCK for columns in SPLITS]
+    y_first, z_blocks = sum(counts), Z_FIRST // BLOCK
+
+    def kernel(place_ref, rows_ref, w_ref, up_ref, down_ref, *rest):
+        group_refs, (kept_ref, given_ref), held = rest[: len(counts)], rest[len(counts) : -1], rest[-1]
+        block = pl.program_id(0)
+        product = jnp.dot(rows_ref[...], w_ref[...], preferred_element_type=jnp.float32)
+        start = 0
+        for group_ref, count in zip(group_refs, counts):
+
+            @pl.when((block >= start) & (block < start + count))
+            def _(group_ref=group_ref):
+                group_ref[...] = product
+
+            start += count
+
+        @pl.when(block < y_first)
+        def _():
+            held[...] = product
+            first = pl.multiple_of(place_ref[0] * (ZH * own), ZH * own)
+            up_ref[...] = held[pl.ds(first, own), :]
+            down_ref[...] = held[pl.ds(pl.multiple_of(first + own, own), own), :]
+
+        @pl.when(block >= y_first)
+        def _():
+            sides = product.reshape(ring, ZH, own, BLOCK)
+            low, high = sides[:, 0], sides[:, 1]
+            kept_ref[...] = jnp.where(place_ref[1] == 0, low, high)
+            given_ref[...] = jnp.where(place_ref[1] == 0, high, low)
+
+    def spec(height, first, count):
+        return pl.BlockSpec((height, BLOCK), lambda j, p: (0, jnp.clip(j - first, 0, count - 1)))
+
+    starts = [sum(counts[:g]) for g in range(len(counts))]
+    z_spec = pl.BlockSpec((ring, own, BLOCK), lambda j, p: (0, 0, jnp.clip(j - y_first, 0, z_blocks - 1)))
+    f32 = jnp.float32
+    return pl.pallas_call(
+        kernel,
+        grid_spec=pltpu.PrefetchScalarGridSpec(
+            num_scalar_prefetch=1,
+            grid=(y_first + z_blocks,),
+            in_specs=[
+                pl.BlockSpec((tokens, depth), lambda j, p: (0, 0)),
+                pl.BlockSpec((None, depth, BLOCK), lambda j, p: (0, 0, j)),
+            ],
+            out_specs=[spec(own, 0, y_first), spec(own, 0, y_first)]
+            + [spec(tokens, first, count) for first, count in zip(starts, counts)]
+            + [z_spec, z_spec],
+            scratch_shapes=[pltpu.VMEM((tokens, BLOCK), f32)],
+        ),
+        out_shape=[jax.ShapeDtypeStruct((own, y_first * BLOCK), f32)] * 2
+        + [jax.ShapeDtypeStruct((tokens, columns), f32) for columns in SPLITS]
+        + [jax.ShapeDtypeStruct((ring, own, Z_FIRST), f32)] * 2,
+    )(place, rows, weights)
+
+
 def body(attn_out, dest, o_weight, head, coef):
     rows = attn_out[0]
-    matrix = o_weight[0]
-    tokens, width = rows.shape[0], matrix.shape[1]
+    tokens, width = rows.shape[0], o_weight.shape[2]
     zh, y = lax.axis_index("zh"), lax.axis_index("y")
     ring, groups = lax.axis_size("y"), lax.axis_size("dp")
     own = tokens // (ring * ZH)
@@ -49,35 +109,27 @@
     for columns in SPLITS:
         cuts.append(cuts[-1] + columns)
     spans = range(len(SPLITS))
-    parts, ups, downs = [], [], []
 
     def owned_by(g, owner):
         return lax.dynamic_index_in_dim(parts[g], owner % ring, 0, False)
 
-    for g in spans:
-        product = jnp.dot(after_last(rows), matrix[:, cuts[g] : cuts[g + 1]], preferred_element_type=jnp.float32)
-        parts.append(product.reshape(ring, ZH, own, SPLITS[g]))
-        opposite = owned_by(g, y + far)
-        ups.append(along(opposite[0], 1)[None])
-        downs.append(along(opposite[1], -1)[None])
-
-    def z_sides(value):
-        return jnp.where(zh == 0, value[:, 0], value[:, 1]), jnp.where(zh == 0, value[:, 1], value[:, 0])
+    place = jnp.stack([(y + far) % ring, zh]).astype(jnp.int32)
+    up_first, down_first, *parts, kept, given = products(rows, o_weight, place, ring, own)
+    parts = [part.reshape(ring, ZH, own, part.shape[1]) for part in parts]
+    ups = [along(up_first, 1)[None]] * len(SPLITS)
+    downs = [along(down_first, -1)[None]] * len(SPLITS)
+    received = ship(given, "zh", swap)
+    z_summed = kept + received
 
     for step in range(far - 1, 0, -1):
         for g in spans:
-            if step == far - 1 and g == 1:
-                product = jnp.dot(after_last(rows), matrix[:, cuts[-1] :], preferred_element_type=jnp.float32)
-                kept, given = z_sides(product.reshape(ring, ZH, own, Z_FIRST))
-                received = ship(given, "zh", swap)
-                z_summed = kept + received
             up = after_last(ups[g])
             if step == far - 1:
-                up = lax.pad(up, 0.0, ((0, 1, 0), (0, 0, 0), (0, 0, 0)))
+                up = lax.pad(up[:, :, cuts[g] : cuts[g + 1]], 0.0, ((0, 1, 0), (0, 0, 0), (0, 0, 0)))
             ups[g] = along(join(owned_by(g, y + step), up), 1)
             down = after_last(downs[g])
             if step == far - 1:
-                down = lax.pad(down, 0.0, ((1, 0, 0), (0, 0, 0), (0, 0, 0)))
+                down = lax.pad(down[:, :, cuts[g] : cuts[g + 1]], 0.0, ((1, 0, 0), (0, 0, 0), (0, 0, 0)))
             downs[g] = along(join(owned_by(g, y - step), down), -1)
 
     gain = head[0].astype(jnp.float32)
@@ -92,13 +144,11 @@
         kept = jnp.where(zh == 0, total[0], total[1])
         given = jnp.where(zh == 0, total[1], total[0])
         done.append((kept + ship(given, "zh", swap), cuts[g], cuts[g + 1]))
-        if g == 0:
-            sent.append(given)
-            turned = lax.all_to_all(z_summed, "y", 0, 0, tiled=True)
+    turned = lax.all_to_all(z_summed, "y", 0, 0, tiled=True)
     done.append((jnp.sum(turned, axis=0), cuts[-1], width))
     for full, first, last in done:
-        square, product = measured(full, first, last)
-        squares, numer = squares + square, numer + product
+        square, weighted = measured(full, first, last)
+        squares, numer = squares + square, numer + weighted
     score = coef[0] * numer * lax.rsqrt(squares / width + 1e-05)
 
     names = jnp.arange(groups, dtype=jnp.int32)[None, :]

time: 205 us -> 223 us (1.088)
  Pallas kernels: 0 us -> 16 us
  matrix products: 7.98 us -> 0 us
  waiting for transfers between devices: 38.6 us -> 43.8 us
    pallas_call x0 -> x1, Pallas kernels: none -> 16 us  [products(): pl.pallas_call(kernel, grid_spec=pltpu.PrefetchScalarGridSpec(num_scalar_...]
    dot_general x3 -> x0, matrix products: 7.98 us -> none  [the longest x2 6.16 us: body(): jnp.dot(after_last(rows), matrix[:, cuts[g]:cuts[g + 1]], preferred_eleme...]
    all_to_all x2, starting transfers between devices: 49.5 us -> 57.3 us  [everyone(): return lax.all_to_all(copies, axes, 0, 0, tiled=True)]
    ppermute x19 -> x17, starting transfers between devices: 79.7 us -> 73.3 us  [ship(): return lax.ppermute(value, axis, pairs)]
    ppermute x19 -> x17, waiting for transfers between devices: 20.6 us -> 25.8 us  [ship(): return lax.ppermute(value, axis, pairs)]
  transfers between devices with their start and end apart: 22 -> 20, of which waited for: 8 -> 7; matrix products, arithmetic and copies ran while one was open for 9% -> 8% of each run, Pallas kernels for 0% -> 0%
where the time goes in v2:
time: 223 us; the launch traced here: 221 us
  starting transfers between devices  137 us (61%)
  waiting for transfers between devices  43.8 us (20%)
  other arithmetic  17.6 us (8%)
  Pallas kernels  16 us (7%)
  local copies, waits for them, and re-layouts  5.57 us (2%)
    ppermute x17, starting transfers between devices, ship(): return lax.ppermute(value, axis, pairs)  73.3 us
    all_to_all x2, starting transfers between devices, everyone(): return lax.all_to_all(copies, axes, 0, 0, tiled=True)  57.3 us
    ppermute x17, waiting for transfers between devices, ship(): return lax.ppermute(value, axis, pairs)  25.8 us
    all_to_all x2, waiting for transfers between devices, everyone(): return lax.all_to_all(copies, axes, 0, 0, tiled=True)  18 us
    pallas_call x1, Pallas kernels, products(): pl.pallas_call(kernel, grid_spec=pltpu.PrefetchScalarGridSpec(num_scalar_...  16 us
    add x14, other arithmetic, join(): total = total + value  13.7 us
    all_to_all x1, starting transfers between devices, body(): turned = lax.all_to_all(z_summed, 'y', 0, 0, tiled=True)  6.3 us
  transfers between devices with their start and end apart: 20, of which 7 were waited for; matrix products, arithmetic and copies ran while one was open for 8% of the time, Pallas kernels for 0%

profile of v2, /device:TPU:1, one launch (start us, length us, event | category | flops | bytes accessed | tf_op | source)
XLA Modules:
  0.0 221.1 jit_solution(10781250833738616834)
XLA Ops:
  0.0 0.6 pad_add_fusion.place_ref
  0.6 16.0 %shard_map.55 = (f32[16,6656]{1,0:T(8,128)}, f32[16,6656]{1,0:T(8,128)}, f32[256,3584]{1,0:T(8,128)}, f32[256,3072]{1,0:T(8,128)}, f32[8,16,1536]{2,1,0:T(8,128)}, /*index=5*/f32[8,16,1536]{2,1,0:T(8,128)}) custom-call(s32[2]{0:T(128)} %pad_add_fusion.place_ref, bf16[256,512]{1,0:T(8,128)(2,1)} %bitcast.77, bf16[1,512,8192]{2,1,0:T(8,128)(2,1)} %w_ref.1), custom_call_target="tpu_custom_call" | custom-call | tf_op jit(solution)/shard_map/pallas_call | solution.py:61
  16.6 4.1 %collective-permute-start = (f32[16,6656]{1,0:T(8,128)}, f32[16,6656]{1,0:T(8,128)S(1)}, u32[]{:S(2)}, u32[]{:S(2)}) collective-permute-start(f32[16,6656]{1,0:T(8,128)} %get-tuple-element.26), channel_id=1, source_target_pairs={{0,4},{4,8},{8,12},{12,16},{16,20},{20,24},{24,28},{28,0},{1,5},{5... | collective-permute-start | bytes 1277960 | tf_op jit(solution)/shard_map/ppermute | solution.py:100
  20.7 3.8 %collective-permute-start.2 = (f32[16,6656]{1,0:T(8,128)}, f32[16,6656]{1,0:T(8,128)S(1)}, u32[]{:S(2)}, u32[]{:S(2)}) collective-permute-start(f32[16,6656]{1,0:T(8,128)} %get-tuple-element.30), channel_id=1, source_target_pairs={{0,28},{4,0},{8,4},{12,8},{16,12},{20,16},{24,20},{28,24},{1,29},{... | collective-permute-start | bytes 1277960 | tf_op jit(solution)/shard_map/ppermute | solution.py:100
  24.6 14.9 %collective-permute-start.16 = (f32[8,16,1536]{2,1,0:T(8,128)}, f32[8,16,1536]{2,1,0:T(8,128)S(1)}, u32[]{:S(2)}, u32[]{:S(2)}) collective-permute-start(f32[8,16,1536]{2,1,0:T(8,128)} %get-tuple-element.27), channel_id=1, source_target_pairs={{0,32},{32,0},{1,33},{33,1},{2,34},{34,2},{3,35},{35,3},{4,36},{36... | collective-permute-start | bytes 2359304 | tf_op jit(solution)/shard_map/ppermute | solution.py:100
  40.4 0.8 copy-done.3
  41.1 1.1 bitcast_add_fusion.3
  42.2 1.9 collective-permute-start.1
  44.1 0.8 copy-done.2
  45.0 1.1 bitcast_add_fusion.2
  46.0 4.6 %collective-permute-start.6 = (f32[2,16,3584]{2,1,0:T(8,128)S(1)}, f32[2,16,3584]{2,1,0:T(8,128)S(1)}, u32[]{:S(2)}, u32[]{:S(2)}) collective-permute-start(f32[2,16,3584]{2,1,0:T(8,128)S(1)} %bitcast_add_fusion.2), channel_id=1, source_target_pairs={{0,28},{4,0},{8,4},{12,8},{16,12},{20,16},{24,20},{28,24},{1,29},{... | collective-permute-start | bytes 1376264 | tf_op jit(solution)/shard_map/ppermute | solution.py:100
  50.6 0.9 slice.63
  51.6 1.8 bitcast_add_fusion.12
  53.4 1.9 collective-permute-start.5
  55.3 0.9 slice.64
  56.3 1.8 bitcast_add_fusion.13
  58.0 4.6 %collective-permute-start.4 = (f32[2,16,3072]{2,1,0:T(8,128)}, f32[2,16,3072]{2,1,0:T(8,128)}, u32[]{:S(2)}, u32[]{:S(2)}) collective-permute-start(f32[2,16,3072]{2,1,0:T(8,128)} %bitcast_add_fusion.13), channel_id=1, source_target_pairs={{0,28},{4,0},{8,4},{12,8},{16,12},{20,16},{24,20},{28,24},{1,29},{... | collective-permute-start | bytes 1179656 | tf_op jit(solution)/shard_map/ppermute | solution.py:100
  62.6 1.0 add.209
  63.6 6.3 %all-to-all-start = ((f32[8,16,1536]{2,1,0:T(8,128)}), f32[8,16,1536]{2,1,0:T(8,128)S(1)}, u32[]{:S(2)}, u32[]{:S(2)}) async-start(f32[8,16,1536]{2,1,0:T(8,128)} %add.209), calls=%async_computation | async-start | bytes 1572864 | tf_op jit(solution)/shard_map/all_to_all | solution.py:147
  69.9 1.2 bitcast_add_fusion.4
  71.2 3.4 %collective-permute-start.3 = (f32[2,16,3584]{2,1,0:T(8,128)S(1)}, f32[2,16,3584]{2,1,0:T(8,128)S(1)}, u32[]{:S(2)}, u32[]{:S(2)}) collective-permute-start(f32[2,16,3584]{2,1,0:T(8,128)S(1)} %bitcast_add_fusion.4), channel_id=1, source_target_pairs={{0,4},{4,8},{8,12},{12,16},{16,20},{20,24},{24,28},{28,0},{1,5},{5... | collective-permute-start | bytes 1376264 | tf_op jit(solution)/shard_map/ppermute | solution.py:100
  74.5 1.1 bitcast_add_fusion.1
  75.6 3.1 %collective-permute-start.10 = (f32[2,16,3584]{2,1,0:T(8,128)S(1)}, f32[2,16,3584]{2,1,0:T(8,128)S(1)}, u32[]{:S(2)}, u32[]{:S(2)}) collective-permute-start(f32[2,16,3584]{2,1,0:T(8,128)S(1)} %bitcast_add_fusion.1), channel_id=1, source_target_pairs={{0,28},{4,0},{8,4},{12,8},{16,12},{20,16},{24,20},{28,24},{1,29},{... | collective-permute-start | bytes 1376264 | tf_op jit(solution)/shard_map/ppermute | solution.py:100
  78.8 1.2 bitcast_add_fusion.10
  79.9 2.1 collective-permute-start.9
  82.1 1.0 bitcast_add_fusion.11
  83.2 4.3 %collective-permute-start.8 = (f32[2,16,3072]{2,1,0:T(8,128)S(1)}, f32[2,16,3072]{2,1,0:T(8,128)S(1)}, u32[]{:S(2)}, u32[]{:S(2)}) collective-permute-start(f32[2,16,3072]{2,1,0:T(8,128)S(1)} %bitcast_add_fusion.11), channel_id=1, source_target_pairs={{0,28},{4,0},{8,4},{12,8},{16,12},{20,16},{24,20},{28,24},{1,29},{... | collective-permute-start | bytes 1179656 | tf_op jit(solution)/shard_map/ppermute | solution.py:100
  87.5 12.2 %collective-permute-done.3 = f32[2,16,3584]{2,1,0:T(8,128)S(1)} collective-permute-done((f32[2,16,3584]{2,1,0:T(8,128)S(1)}, f32[2,16,3584]{2,1,0:T(8,128)S(1)}, u32[]{:S(2)}, u32[]{:S(2)}) %collective-permute-start.3) | collective-permute-done | bytes 458784 | tf_op jit(solution)/shard_map/ppermute | solution.py:100
  99.7 1.1 bitcast_add_fusion.5
  100.8 1.9 collective-permute-start.7
  102.7 1.1 bitcast_add_fusion
  103.8 4.6 %collective-permute-start.11 = (f32[2,16,3584]{2,1,0:T(8,128)S(1)}, f32[2,16,3584]{2,1,0:T(8,128)S(1)}, u32[]{:S(2)}, u32[]{:S(2)}) collective-permute-start(f32[2,16,3584]{2,1,0:T(8,128)S(1)} %bitcast_add_fusion), channel_id=1, source_target_pairs={{0,28},{4,0},{8,4},{12,8},{16,12},{20,16},{24,20},{28,24},{1,29},{... | collective-permute-start | bytes 1376264 | tf_op jit(solution)/shard_map/ppermute | solution.py:100
  108.5 1.9 collective-permute-start.13
  110.5 4.6 %collective-permute-start.14 = (f32[2,16,3072]{2,1,0:T(8,128)S(1)}, f32[2,16,3072]{2,1,0:T(8,128)S(1)}, u32[]{:S(2)}, u32[]{:S(2)}) collective-permute-start(f32[2,16,3072]{2,1,0:T(8,128)S(1)} %bitcast_add_fusion.9), channel_id=1, source_target_pairs={{0,28},{4,0},{8,4},{12,8},{16,12},{20,16},{24,20},{28,24},{1,29},{... | collective-permute-start | bytes 1179656 | tf_op jit(solution)/shard_map/ppermute | solution.py:100
  115.1 2.9 %collective-permute-done.7 = f32[2,16,3584]{2,1,0:T(8,128)S(1)} collective-permute-done((f32[2,16,3584]{2,1,0:T(8,128)S(1)}, f32[2,16,3584]{2,1,0:T(8,128)S(1)}, u32[]{:S(2)}, u32[]{:S(2)}) %collective-permute-start.7) | collective-permute-done | bytes 458784 | tf_op jit(solution)/shard_map/ppermute | solution.py:100
  118.0 1.1 fusion
  119.1 7.3 %collective-permute-done.13 = f32[2,16,3072]{2,1,0:T(8,128)S(1)} collective-permute-done((f32[2,16,3072]{2,1,0:T(8,128)S(1)}, f32[2,16,3072]{2,1,0:T(8,128)S(1)}, u32[]{:S(2)}, u32[]{:S(2)}) %collective-permute-start.13) | collective-permute-done | bytes 393248 | tf_op jit(solution)/shard_map/ppermute | solution.py:100
  126.5 1.9 collective-permute-start.15
  128.5 9.7 %collective-permute-start.12 = (f32[16,3584]{1,0:T(8,128)S(1)}, f32[16,3584]{1,0:T(8,128)S(1)}, u32[]{:S(2)}, u32[]{:S(2)}) collective-permute-start(f32[16,3584]{1,0:T(8,128)S(1)} %select_bitcast_fusion), channel_id=1, source_target_pairs={{0,32},{32,0},{1,33},{33,1},{2,34},{34,2},{3,35},{35,3},{4,36},{36... | collective-permute-start | bytes 688136 | tf_op jit(solution)/shard_map/ppermute | solution.py:100
  138.2 1.0 collective-permute-done.15
  139.4 2.3 %collective-permute-done.12 = f32[16,3584]{1,0:T(8,128)S(1)} collective-permute-done((f32[16,3584]{1,0:T(8,128)S(1)}, f32[16,3584]{1,0:T(8,128)S(1)}, u32[]{:S(2)}, u32[]{:S(2)}) %collective-permute-start.12) | collective-permute-done | bytes 229408 | tf_op jit(solution)/shard_map/ppermute | solution.py:100
  142.1 0.6 broadcast_in_dim.10
  142.7 50.0 %all-to-all-start.1 = ((f32[24,1,128]{2,1,0:T(1,128)}), f32[24,1,128]{2,1,0:T(1,128)S(1)}, u32[]{:S(2)}, u32[]{:S(2)}) async-start(f32[24,1,128]{2,1,0:T(1,128)} %broadcast_in_dim.10), calls=%async_computation.1 | async-start | bytes 24576 | tf_op jit(solution)/shard_map/all_to_all | solution.py:20
  192.8 9.3 %all-to-all-done.1 = f32[24,1,128]{2,1,0:T(1,128)S(1)} async-done(((f32[24,1,128]{2,1,0:T(1,128)}), f32[24,1,128]{2,1,0:T(1,128)S(1)}, u32[]{:S(2)}, u32[]{:S(2)}) %all-to-all-start.1) | async-done | bytes 12320 | tf_op jit(solution)/shard_map/all_to_all | solution.py:20
  202.6 0.7 reduce.7
  203.6 0.6 broadcast_in_dim.11
  204.3 7.3 %all-to-all-start.2 = ((f32[32,1,128]{2,1,0:T(1,128)}), f32[32,1,128]{2,1,0:T(1,128)S(1)}, u32[]{:S(2)}, u32[]{:S(2)}) async-start(f32[32,1,128]{2,1,0:T(1,128)} %broadcast_in_dim.11), calls=%async_computation.2 | async-start | bytes 32768 | tf_op jit(solution)/shard_map/all_to_all | solution.py:20
  211.6 8.7 %all-to-all-done.2 = f32[32,1,128]{2,1,0:T(1,128)S(1)} async-done(((f32[32,1,128]{2,1,0:T(1,128)}), f32[32,1,128]{2,1,0:T(1,128)S(1)}, u32[]{:S(2)}, u32[]{:S(2)}) %all-to-all-start.2) | async-done | bytes 16416 | tf_op jit(solution)/shard_map/all_to_all | solution.py:20
  (53 shorter events, 2.8 us)
Async XLA Ops:
  0.6 39.0 %copy-start.4 = (bf16[1,8192]{1,0:T(2,128)(2,1)S(1)}, bf16[1,8192]{1,0:T(2,128)(2,1)}, u32[]{:S(2)}) copy-start(bf16[1,8192]{1,0:T(2,128)(2,1)} %param.8) | copy-start | bytes 49156
  16.6 46.0 %copy-start.1 = (f32[8,16,1536]{2,1,0:T(8,128)S(1)}, f32[8,16,1536]{2,1,0:T(8,128)}, u32[]{:S(2)}) copy-start(f32[8,16,1536]{2,1,0:T(8,128)} %get-tuple-element.44) | copy-start | bytes 2359300
  16.6 23.7 %collective-permute-start = (f32[16,6656]{1,0:T(8,128)}, f32[16,6656]{1,0:T(8,128)S(1)}, u32[]{:S(2)}, u32[]{:S(2)}) collective-permute-start(f32[16,6656]{1,0:T(8,128)} %get-tuple-element.26), channel_id=1, source_target_pairs={{0,4},{4,8},{8,12},{12,16},{16,20},{20,24},{24,28},{28,0},{1,5},{5... | collective-permute-start | bytes 1277960 | tf_op jit(solution)/shard_map/ppermute | solution.py:100
  20.7 23.4 %collective-permute-start.2 = (f32[16,6656]{1,0:T(8,128)}, f32[16,6656]{1,0:T(8,128)S(1)}, u32[]{:S(2)}, u32[]{:S(2)}) collective-permute-start(f32[16,6656]{1,0:T(8,128)} %get-tuple-element.30), channel_id=1, source_target_pairs={{0,28},{4,0},{8,4},{12,8},{16,12},{20,16},{24,20},{28,24},{1,29},{... | collective-permute-start | bytes 1277960 | tf_op jit(solution)/shard_map/ppermute | solution.py:100
  24.6 38.0 %collective-permute-start.16 = (f32[8,16,1536]{2,1,0:T(8,128)}, f32[8,16,1536]{2,1,0:T(8,128)S(1)}, u32[]{:S(2)}, u32[]{:S(2)}) collective-permute-start(f32[8,16,1536]{2,1,0:T(8,128)} %get-tuple-element.27), channel_id=1, source_target_pairs={{0,32},{32,0},{1,33},{33,1},{2,34},{34,2},{3,35},{35,3},{4,36},{36... | collective-permute-start | bytes 2359304 | tf_op jit(solution)/shard_map/ppermute | solution.py:100
  40.3 0.8 copy-start.3
  42.2 27.7 %collective-permute-start.1 = (f32[2,16,3584]{2,1,0:T(8,128)S(1)}, f32[2,16,3584]{2,1,0:T(8,128)S(1)}, u32[]{:S(2)}, u32[]{:S(2)}) collective-permute-start(f32[2,16,3584]{2,1,0:T(8,128)S(1)} %bitcast_add_fusion.3), channel_id=1, source_target_pairs={{0,4},{4,8},{8,12},{12,16},{16,20},{20,24},{24,28},{28,0},{1,5},{5... | collective-permute-start | bytes 1376264 | tf_op jit(solution)/shard_map/ppermute | solution.py:100
  44.1 0.8 copy-start.2
  46.0 28.5 %collective-permute-start.6 = (f32[2,16,3584]{2,1,0:T(8,128)S(1)}, f32[2,16,3584]{2,1,0:T(8,128)S(1)}, u32[]{:S(2)}, u32[]{:S(2)}) collective-permute-start(f32[2,16,3584]{2,1,0:T(8,128)S(1)} %bitcast_add_fusion.2), channel_id=1, source_target_pairs={{0,28},{4,0},{8,4},{12,8},{16,12},{20,16},{24,20},{28,24},{1,29},{... | collective-permute-start | bytes 1376264 | tf_op jit(solution)/shard_map/ppermute | solution.py:100
  53.4 25.4 %collective-permute-start.5 = (f32[2,16,3072]{2,1,0:T(8,128)}, f32[2,16,3072]{2,1,0:T(8,128)}, u32[]{:S(2)}, u32[]{:S(2)}) collective-permute-start(f32[2,16,3072]{2,1,0:T(8,128)} %bitcast_add_fusion.12), channel_id=1, source_target_pairs={{0,4},{4,8},{8,12},{12,16},{16,20},{20,24},{24,28},{28,0},{1,5},{5... | collective-permute-start | bytes 1179656 | tf_op jit(solution)/shard_map/ppermute | solution.py:100
  58.0 24.0 %collective-permute-start.4 = (f32[2,16,3072]{2,1,0:T(8,128)}, f32[2,16,3072]{2,1,0:T(8,128)}, u32[]{:S(2)}, u32[]{:S(2)}) collective-permute-start(f32[2,16,3072]{2,1,0:T(8,128)} %bitcast_add_fusion.13), channel_id=1, source_target_pairs={{0,28},{4,0},{8,4},{12,8},{16,12},{20,16},{24,20},{28,24},{1,29},{... | collective-permute-start | bytes 1179656 | tf_op jit(solution)/shard_map/ppermute | solution.py:100
  63.6 78.2 %all-to-all-start = ((f32[8,16,1536]{2,1,0:T(8,128)}), f32[8,16,1536]{2,1,0:T(8,128)S(1)}, u32[]{:S(2)}, u32[]{:S(2)}) async-start(f32[8,16,1536]{2,1,0:T(8,128)} %add.209), calls=%async_computation | async-start | bytes 1572864 | tf_op jit(solution)/shard_map/all_to_all | solution.py:147
  69.9 12.2 %copy-start = (f32[256,3072]{1,0:T(8,128)S(1)}, f32[256,3072]{1,0:T(8,128)}, u32[]{:S(2)}) copy-start(f32[256,3072]{1,0:T(8,128)} %get-tuple-element.29) | copy-start | bytes 9437188
  71.2 28.6 %collective-permute-start.3 = (f32[2,16,3584]{2,1,0:T(8,128)S(1)}, f32[2,16,3584]{2,1,0:T(8,128)S(1)}, u32[]{:S(2)}, u32[]{:S(2)}) collective-permute-start(f32[2,16,3584]{2,1,0:T(8,128)S(1)} %bitcast_add_fusion.4), channel_id=1, source_target_pairs={{0,4},{4,8},{8,12},{12,16},{16,20},{20,24},{24,28},{28,0},{1,5},{5... | collective-permute-start | bytes 1376264 | tf_op jit(solution)/shard_map/ppermute | solution.py:100
  75.6 27.1 %collective-permute-start.10 = (f32[2,16,3584]{2,1,0:T(8,128)S(1)}, f32[2,16,3584]{2,1,0:T(8,128)S(1)}, u32[]{:S(2)}, u32[]{:S(2)}) collective-permute-start(f32[2,16,3584]{2,1,0:T(8,128)S(1)} %bitcast_add_fusion.1), channel_id=1, source_target_pairs={{0,28},{4,0},{8,4},{12,8},{16,12},{20,16},{24,20},{28,24},{1,29},{... | collective-permute-start | bytes 1376264 | tf_op jit(solution)/shard_map/ppermute | solution.py:100
  79.9 28.5 %collective-permute-start.9 = (f32[2,16,3072]{2,1,0:T(8,128)S(1)}, f32[2,16,3072]{2,1,0:T(8,128)S(1)}, u32[]{:S(2)}, u32[]{:S(2)}) collective-permute-start(f32[2,16,3072]{2,1,0:T(8,128)S(1)} %bitcast_add_fusion.10), channel_id=1, source_target_pairs={{0,4},{4,8},{8,12},{12,16},{16,20},{20,24},{24,28},{28,0},{1,5},{5... | collective-permute-start | bytes 1179656 | tf_op jit(solution)/shard_map/ppermute | solution.py:100
  83.2 27.3 %collective-permute-start.8 = (f32[2,16,3072]{2,1,0:T(8,128)S(1)}, f32[2,16,3072]{2,1,0:T(8,128)S(1)}, u32[]{:S(2)}, u32[]{:S(2)}) collective-permute-start(f32[2,16,3072]{2,1,0:T(8,128)S(1)} %bitcast_add_fusion.11), channel_id=1, source_target_pairs={{0,28},{4,0},{8,4},{12,8},{16,12},{20,16},{24,20},{28,24},{1,29},{... | collective-permute-start | bytes 1179656 | tf_op jit(solution)/shard_map/ppermute | solution.py:100
  100.8 17.2 %collective-permute-start.7 = (f32[2,16,3584]{2,1,0:T(8,128)S(1)}, f32[2,16,3584]{2,1,0:T(8,128)S(1)}, u32[]{:S(2)}, u32[]{:S(2)}) collective-permute-start(f32[2,16,3584]{2,1,0:T(8,128)S(1)} %bitcast_add_fusion.5), channel_id=1, source_target_pairs={{0,4},{4,8},{8,12},{12,16},{16,20},{20,24},{24,28},{28,0},{1,5},{5... | collective-permute-start | bytes 1376264 | tf_op jit(solution)/shard_map/ppermute | solution.py:100
  103.8 14.1 %collective-permute-start.11 = (f32[2,16,3584]{2,1,0:T(8,128)S(1)}, f32[2,16,3584]{2,1,0:T(8,128)S(1)}, u32[]{:S(2)}, u32[]{:S(2)}) collective-permute-start(f32[2,16,3584]{2,1,0:T(8,128)S(1)} %bitcast_add_fusion), channel_id=1, source_target_pairs={{0,28},{4,0},{8,4},{12,8},{16,12},{20,16},{24,20},{28,24},{1,29},{... | collective-permute-start | bytes 1376264 | tf_op jit(solution)/shard_map/ppermute | solution.py:100
  108.5 17.9 %collective-permute-start.13 = (f32[2,16,3072]{2,1,0:T(8,128)S(1)}, f32[2,16,3072]{2,1,0:T(8,128)S(1)}, u32[]{:S(2)}, u32[]{:S(2)}) collective-permute-start(f32[2,16,3072]{2,1,0:T(8,128)S(1)} %bitcast_add_fusion.8), channel_id=1, source_target_pairs={{0,4},{4,8},{8,12},{12,16},{16,20},{20,24},{24,28},{28,0},{1,5},{5... | collective-permute-start | bytes 1179656 | tf_op jit(solution)/shard_map/ppermute | solution.py:100
  110.5 82.2 %copy-start.5 = (s32[256,1]{0,1:T(1,128)S(1)}, s32[256,1]{0,1:T(1,128)}, u32[]{:S(2)}) copy-start(s32[256,1]{0,1:T(1,128)} %param.6) | copy-start | bytes 3076
  110.5 15.9 %collective-permute-start.14 = (f32[2,16,3072]{2,1,0:T(8,128)S(1)}, f32[2,16,3072]{2,1,0:T(8,128)S(1)}, u32[]{:S(2)}, u32[]{:S(2)}) collective-permute-start(f32[2,16,3072]{2,1,0:T(8,128)S(1)} %bitcast_add_fusion.9), channel_id=1, source_target_pairs={{0,28},{4,0},{8,4},{12,8},{16,12},{20,16},{24,20},{28,24},{1,29},{... | collective-permute-start | bytes 1179656 | tf_op jit(solution)/shard_map/ppermute | solution.py:100
  126.5 12.7 %collective-permute-start.15 = (f32[16,3072]{1,0:T(8,128)S(1)}, f32[16,3072]{1,0:T(8,128)S(1)}, u32[]{:S(2)}, u32[]{:S(2)}) collective-permute-start(f32[16,3072]{1,0:T(8,128)S(1)} %select_bitcast_fusion.1), channel_id=1, source_target_pairs={{0,32},{32,0},{1,33},{33,1},{2,34},{34,2},{3,35},{35,3},{4,36},{36... | collective-permute-start | bytes 589832 | tf_op jit(solution)/shard_map/ppermute | solution.py:100
  128.5 13.2 %collective-permute-start.12 = (f32[16,3584]{1,0:T(8,128)S(1)}, f32[16,3584]{1,0:T(8,128)S(1)}, u32[]{:S(2)}, u32[]{:S(2)}) collective-permute-start(f32[16,3584]{1,0:T(8,128)S(1)} %select_bitcast_fusion), channel_id=1, source_target_pairs={{0,32},{32,0},{1,33},{33,1},{2,34},{34,2},{3,35},{35,3},{4,36},{36... | collective-permute-start | bytes 688136 | tf_op jit(solution)/shard_map/ppermute | solution.py:100
  142.7 59.4 %all-to-all-start.1 = ((f32[24,1,128]{2,1,0:T(1,128)}), f32[24,1,128]{2,1,0:T(1,128)S(1)}, u32[]{:S(2)}, u32[]{:S(2)}) async-start(f32[24,1,128]{2,1,0:T(1,128)} %broadcast_in_dim.10), calls=%async_computation.1 | async-start | bytes 24576 | tf_op jit(solution)/shard_map/all_to_all | solution.py:20
  204.3 16.0 %all-to-all-start.2 = ((f32[32,1,128]{2,1,0:T(1,128)}), f32[32,1,128]{2,1,0:T(1,128)S(1)}, u32[]{:S(2)}, u32[]{:S(2)}) async-start(f32[32,1,128]{2,1,0:T(1,128)} %broadcast_in_dim.11), calls=%async_computation.2 | async-start | bytes 32768 | tf_op jit(solution)/shard_map/all_to_all | solution.py:20

commit v3 on v1

--- a/solution.py
+++ b/solution.py
@@ -54,12 +54,19 @@
     def owned_by(g, owner):
         return lax.dynamic_index_in_dim(parts[g], owner % ring, 0, False)
 
-    for g in spans:
+    columns = cuts[-1]
+    opposite_rows = lax.dynamic_slice_in_dim(rows, (y + far) % ring * (ZH * own), ZH * own)
+    opposite = jnp.dot(opposite_rows, matrix[:, :columns], preferred_element_type=jnp.float32)
+    up_first = along(opposite[:own], 1)[None]
+    down_first = along(opposite[own:], -1)[None]
+
+    def group_product(g):
         product = jnp.dot(after_last(rows), matrix[:, cuts[g] : cuts[g + 1]], preferred_element_type=jnp.float32)
         parts.append(product.reshape(ring, ZH, own, SPLITS[g]))
-        opposite = owned_by(g, y + far)
-        ups.append(along(opposite[0], 1)[None])
-        downs.append(along(opposite[1], -1)[None])
+        ups.append(up_first)
+        downs.append(down_first)
+
+    group_product(0)
 
     def z_sides(value):
         return jnp.where(zh == 0, value[:, 0], value[:, 1]), jnp.where(zh == 0, value[:, 1], value[:, 0])
@@ -67,17 +74,18 @@
     for step in range(far - 1, 0, -1):
         for g in spans:
             if step == far - 1 and g == 1:
-                product = jnp.dot(after_last(rows), matrix[:, cuts[-1] :], preferred_element_type=jnp.float32)
-                kept, given = z_sides(product.reshape(ring, ZH, own, Z_FIRST))
+                group_product(1)
+                z_product = jnp.dot(after_last(rows), matrix[:, columns:], preferred_element_type=jnp.float32)
+                kept, given = z_sides(z_product.reshape(ring, ZH, own, Z_FIRST))
                 received = ship(given, "zh", swap)
                 z_summed = kept + received
             up = after_last(ups[g])
             if step == far - 1:
-                up = lax.pad(up, 0.0, ((0, 1, 0), (0, 0, 0), (0, 0, 0)))
+                up = lax.pad(up[:, :, cuts[g] : cuts[g + 1]], 0.0, ((0, 1, 0), (0, 0, 0), (0, 0, 0)))
             ups[g] = along(join(owned_by(g, y + step), up), 1)
             down = after_last(downs[g])
             if step == far - 1:
-                down = lax.pad(down, 0.0, ((1, 0, 0), (0, 0, 0), (0, 0, 0)))
+                down = lax.pad(down[:, :, cuts[g] : cuts[g + 1]], 0.0, ((1, 0, 0), (0, 0, 0), (0, 0, 0)))
             downs[g] = along(join(owned_by(g, y - step), down), -1)
 
     gain = head[0].astype(jnp.float32)
@@ -92,13 +100,11 @@
         kept = jnp.where(zh == 0, total[0], total[1])
         given = jnp.where(zh == 0, total[1], total[0])
         done.append((kept + ship(given, "zh", swap), cuts[g], cuts[g + 1]))
-        if g == 0:
-            sent.append(given)
-            turned = lax.all_to_all(z_summed, "y", 0, 0, tiled=True)
+    turned = lax.all_to_all(z_summed, "y", 0, 0, tiled=True)
     done.append((jnp.sum(turned, axis=0), cuts[-1], width))
     for full, first, last in done:
-        square, product = measured(full, first, last)
-        squares, numer = squares + square, numer + product
+        square, weighted = measured(full, first, last)
+        squares, numer = squares + square, numer + weighted
     score = coef[0] * numer * lax.rsqrt(squares / width + 1e-05)
 
     names = jnp.arange(groups, dtype=jnp.int32)[None, :]

time: 205 us -> 200 us (0.976)
  starting transfers between devices: 136 us -> 131 us
  waiting for transfers between devices: 38.6 us -> 42.9 us
  other arithmetic: 15.4 us -> 11.2 us
    ppermute x19 -> x17, waiting for transfers between devices: 20.6 us -> 24.9 us  [ship(): return lax.ppermute(value, axis, pairs)]
    add x14, other arithmetic: 12 us -> 7.83 us  [join(): total = total + value]
    all_to_all x2, starting transfers between devices: 49.5 us -> 47.3 us  [everyone(): return lax.all_to_all(copies, axes, 0, 0, tiled=True)]
    ppermute x19 -> x17, starting transfers between devices: 79.7 us -> 77.6 us  [ship(): return lax.ppermute(value, axis, pairs)]
    dot_general x3 -> x4, matrix products: 7.98 us -> 9.18 us  [the longest x2 4.35 us: group_product(): jnp.dot(after_last(rows), matrix[:, cuts[g]:cuts[g + 1]], preferred_eleme...]
  transfers between devices with their start and end apart: 22 -> 20, of which waited for: 8 -> 9; matrix products, arithmetic and copies ran while one was open for 9% -> 7% of each run, Pallas kernels for 0% -> 0%
where the time goes in v3:
time: 200 us; the launch traced here: 199 us
  starting transfers between devices  131 us (66%)
  waiting for transfers between devices  42.9 us (21%)
  other arithmetic  11.2 us (6%)
  matrix products  9.18 us (5%)
  local copies, waits for them, and re-layouts  3.19 us (2%)
    ppermute x17, starting transfers between devices, ship(): return lax.ppermute(value, axis, pairs)  77.6 us
    all_to_all x2, starting transfers between devices, everyone(): return lax.all_to_all(copies, axes, 0, 0, tiled=True)  47.3 us
    ppermute x17, waiting for transfers between devices, ship(): return lax.ppermute(value, axis, pairs)  24.9 us
    all_to_all x2, waiting for transfers between devices, everyone(): return lax.all_to_all(copies, axes, 0, 0, tiled=True)  18 us
    add x14, other arithmetic, join(): total = total + value  7.83 us
    all_to_all x1, starting transfers between devices, body(): turned = lax.all_to_all(z_summed, 'y', 0, 0, tiled=True)  6.02 us
    dot_general x2, matrix products, group_product(): jnp.dot(after_last(rows), matrix[:, cuts[g]:cuts[g + 1]], preferred_eleme...  4.35 us
    dot_general x1, matrix products, body(): jnp.dot(opposite_rows, matrix[:, :columns], preferred_element_type=jnp.fl...  4.32 us
  transfers between devices with their start and end apart: 20, of which 9 were waited for; matrix products, arithmetic and copies ran while one was open for 7% of the time, Pallas kernels for 0%

profile of v3, /device:TPU:1, one launch (start us, length us, event | category | flops | bytes accessed | tf_op | source)
XLA Modules:
  0.0 198.6 jit_solution(14523864673597115065)
XLA Ops:
  0.0 0.9 copy-done
  1.0 4.3 %fusion = f32[32,6912]{1,0:T(8,128)S(1)} fusion(bf16[512,8192]{1,0:T(8,128)(2,1)} %bitcast.81, bf16[1,256,512]{2,1,0:T(8,128)(2,1)S(1)} %copy-done, s32[]{:T(128)S(6)} %select_n.145), kind=kOutput, calls=%fused_computation | convolution fusion | flops 226492416 | bytes 7995396 | tf_op jit(solution)/shard_map/dot_general | solution.py:59
  5.3 4.0 %collective-permute-start = (f32[16,6912]{1,0:T(8,128)S(1)}, f32[16,6912]{1,0:T(8,128)S(1)}, u32[]{:S(2)}, u32[]{:S(2)}) collective-permute-start(f32[16,6912]{1,0:T(8,128)S(1)} %get-tuple-element.45), channel_id=1, source_target_pairs={{0,4},{4,8},{8,12},{12,16},{16,20},{20,24},{24,28},{28,0},{1,5},{5... | collective-permute-start | bytes 1327112 | tf_op jit(solution)/shard_map/ppermute | solution.py:40
  9.4 3.8 %collective-permute-start.2 = (f32[16,6912]{1,0:T(8,128)S(1)}, f32[16,6912]{1,0:T(8,128)S(1)}, u32[]{:S(2)}, u32[]{:S(2)}) collective-permute-start(f32[16,6912]{1,0:T(8,128)S(1)} %get-tuple-element.46), channel_id=1, source_target_pairs={{0,28},{4,0},{8,4},{12,8},{16,12},{20,16},{24,20},{28,24},{1,29},{... | collective-permute-start | bytes 1327112 | tf_op jit(solution)/shard_map/ppermute | solution.py:40
  14.1 3.3 %fusion.2 = f32[256,3584]{1,0:T(8,128)S(1)} fusion(bf16[256,512]{1,0:T(8,128)(2,1)S(1)} %bitcast.78, bf16[512,8192]{1,0:T(8,128)(2,1)} %bitcast.82), kind=kOutput, calls=%fused_computation.2 | convolution fusion | flops 939524096 | bytes 7602176 | tf_op jit(solution)/shard_map/dot_general | solution.py:64
  17.5 0.9 collective-permute-done.2
  18.5 5.9 %collective-permute-start.6 = (f32[2,16,3584]{2,1,0:T(8,128)S(1)}, f32[2,16,3584]{2,1,0:T(8,128)S(1)}, u32[]{:S(2)}, u32[]{:S(2)}) collective-permute-start(f32[2,16,3584]{2,1,0:T(8,128)S(1)} %bitcast_add_fusion.3), channel_id=1, source_target_pairs={{0,28},{4,0},{8,4},{12,8},{16,12},{20,16},{24,20},{28,24},{1,29},{... | collective-permute-start | bytes 1376264 | tf_op jit(solution)/shard_map/ppermute | solution.py:40
  24.4 2.9 %collective-permute-start.1 = (f32[2,16,3584]{2,1,0:T(8,128)S(1)}, f32[2,16,3584]{2,1,0:T(8,128)S(1)}, u32[]{:S(2)}, u32[]{:S(2)}) collective-permute-start(f32[2,16,3584]{2,1,0:T(8,128)S(1)} %bitcast_add_fusion.4), channel_id=1, source_target_pairs={{0,4},{4,8},{8,12},{12,16},{16,20},{20,24},{24,28},{28,0},{1,5},{5... | collective-permute-start | bytes 1376264 | tf_op jit(solution)/shard_map/ppermute | solution.py:40
  27.3 0.5 fusion.6
  27.9 17.0 %collective-permute-start.16 = (f32[8,16,1280]{2,1,0:T(8,128)S(1)}, f32[8,16,1280]{2,1,0:T(8,128)S(1)}, u32[]{:S(2)}, u32[]{:S(2)}) collective-permute-start(f32[8,16,1280]{2,1,0:T(8,128)S(1)} %fusion.8), channel_id=1, source_target_pairs={{0,32},{32,0},{1,33},{33,1},{2,34},{34,2},{3,35},{35,3},{4,36},{36... | collective-permute-start | bytes 1966088 | tf_op jit(solution)/shard_map/ppermute | solution.py:40
  44.8 1.1 fusion.4
  46.0 2.4 %collective-permute-start.5 = (f32[2,16,3328]{2,1,0:T(8,128)S(1)}, f32[2,16,3328]{2,1,0:T(8,128)S(1)}, u32[]{:S(2)}, u32[]{:S(2)}) collective-permute-start(f32[2,16,3328]{2,1,0:T(8,128)S(1)} %bitcast_add_fusion.13), channel_id=1, source_target_pairs={{0,4},{4,8},{8,12},{12,16},{16,20},{20,24},{24,28},{28,0},{1,5},{5... | collective-permute-start | bytes 1277960 | tf_op jit(solution)/shard_map/ppermute | solution.py:40
  48.5 4.1 %collective-permute-start.4 = (f32[2,16,3328]{2,1,0:T(8,128)S(1)}, f32[2,16,3328]{2,1,0:T(8,128)S(1)}, u32[]{:S(2)}, u32[]{:S(2)}) collective-permute-start(f32[2,16,3328]{2,1,0:T(8,128)S(1)} %bitcast_add_fusion.14), channel_id=1, source_target_pairs={{0,28},{4,0},{8,4},{12,8},{16,12},{20,16},{24,20},{28,24},{1,29},{... | collective-permute-start | bytes 1277960 | tf_op jit(solution)/shard_map/ppermute | solution.py:40
  52.6 2.2 %collective-permute-start.3 = (f32[2,16,3584]{2,1,0:T(8,128)S(1)}, f32[2,16,3584]{2,1,0:T(8,128)S(1)}, u32[]{:S(2)}, u32[]{:S(2)}) collective-permute-start(f32[2,16,3584]{2,1,0:T(8,128)S(1)} %bitcast_add_fusion.5), channel_id=1, source_target_pairs={{0,4},{4,8},{8,12},{12,16},{16,20},{20,24},{24,28},{28,0},{1,5},{5... | collective-permute-start | bytes 1376264 | tf_op jit(solution)/shard_map/ppermute | solution.py:40
  54.9 4.3 %collective-permute-start.10 = (f32[2,16,3584]{2,1,0:T(8,128)S(1)}, f32[2,16,3584]{2,1,0:T(8,128)S(1)}, u32[]{:S(2)}, u32[]{:S(2)}) collective-permute-start(f32[2,16,3584]{2,1,0:T(8,128)S(1)} %bitcast_add_fusion.2), channel_id=1, source_target_pairs={{0,28},{4,0},{8,4},{12,8},{16,12},{20,16},{24,20},{28,24},{1,29},{... | collective-permute-start | bytes 1376264 | tf_op jit(solution)/shard_map/ppermute | solution.py:40
  59.3 2.2 %collective-permute-start.9 = (f32[2,16,3328]{2,1,0:T(8,128)S(1)}, f32[2,16,3328]{2,1,0:T(8,128)}, u32[]{:S(2)}, u32[]{:S(2)}) collective-permute-start(f32[2,16,3328]{2,1,0:T(8,128)S(1)} %bitcast_add_fusion.11), channel_id=1, source_target_pairs={{0,4},{4,8},{8,12},{12,16},{16,20},{20,24},{24,28},{28,0},{1,5},{5... | collective-permute-start | bytes 1277960 | tf_op jit(solution)/shard_map/ppermute | solution.py:40
  61.5 0.8 bitcast_add_fusion.12
  62.3 4.3 %collective-permute-start.8 = (f32[2,16,3328]{2,1,0:T(8,128)}, f32[2,16,3328]{2,1,0:T(8,128)}, u32[]{:S(2)}, u32[]{:S(2)}) collective-permute-start(f32[2,16,3328]{2,1,0:T(8,128)} %bitcast_add_fusion.12), channel_id=1, source_target_pairs={{0,28},{4,0},{8,4},{12,8},{16,12},{20,16},{24,20},{28,24},{1,29},{... | collective-permute-start | bytes 1277960 | tf_op jit(solution)/shard_map/ppermute | solution.py:40
  66.6 0.9 bitcast_add_fusion
  67.5 6.0 %all-to-all-start = ((f32[8,16,1280]{2,1,0:T(8,128)}), f32[8,16,1280]{2,1,0:T(8,128)S(1)}, u32[]{:S(2)}, u32[]{:S(2)}) async-start(f32[8,16,1280]{2,1,0:T(8,128)} %bitcast_add_fusion), calls=%async_computation | async-start | bytes 1310720 | tf_op jit(solution)/shard_map/all_to_all | solution.py:103
  73.6 1.1 bitcast_add_fusion.6
  74.6 3.4 %collective-permute-start.7 = (f32[2,16,3584]{2,1,0:T(8,128)S(1)}, f32[2,16,3584]{2,1,0:T(8,128)S(1)}, u32[]{:S(2)}, u32[]{:S(2)}) collective-permute-start(f32[2,16,3584]{2,1,0:T(8,128)S(1)} %bitcast_add_fusion.6), channel_id=1, source_target_pairs={{0,4},{4,8},{8,12},{12,16},{16,20},{20,24},{24,28},{28,0},{1,5},{5... | collective-permute-start | bytes 1376264 | tf_op jit(solution)/shard_map/ppermute | solution.py:40
  78.0 1.1 bitcast_add_fusion.1
  79.1 3.1 %collective-permute-start.11 = (f32[2,16,3584]{2,1,0:T(8,128)S(1)}, f32[2,16,3584]{2,1,0:T(8,128)S(1)}, u32[]{:S(2)}, u32[]{:S(2)}) collective-permute-start(f32[2,16,3584]{2,1,0:T(8,128)S(1)} %bitcast_add_fusion.1), channel_id=1, source_target_pairs={{0,28},{4,0},{8,4},{12,8},{16,12},{20,16},{24,20},{28,24},{1,29},{... | collective-permute-start | bytes 1376264 | tf_op jit(solution)/shard_map/ppermute | solution.py:40
  82.3 1.2 bitcast_add_fusion.9
  83.4 2.1 %collective-permute-start.13 = (f32[2,16,3328]{2,1,0:T(8,128)S(1)}, f32[2,16,3328]{2,1,0:T(8,128)S(1)}, u32[]{:S(2)}, u32[]{:S(2)}) collective-permute-start(f32[2,16,3328]{2,1,0:T(8,128)S(1)} %bitcast_add_fusion.9), channel_id=1, source_target_pairs={{0,4},{4,8},{8,12},{12,16},{16,20},{20,24},{24,28},{28,0},{1,5},{5... | collective-permute-start | bytes 1277960 | tf_op jit(solution)/shard_map/ppermute | solution.py:40
  85.6 1.2 bitcast_add_fusion.10
  86.8 4.3 %collective-permute-start.14 = (f32[2,16,3328]{2,1,0:T(8,128)S(1)}, f32[2,16,3328]{2,1,0:T(8,128)S(1)}, u32[]{:S(2)}, u32[]{:S(2)}) collective-permute-start(f32[2,16,3328]{2,1,0:T(8,128)S(1)} %bitcast_add_fusion.10), channel_id=1, source_target_pairs={{0,28},{4,0},{8,4},{12,8},{16,12},{20,16},{24,20},{28,24},{1,29},{... | collective-permute-start | bytes 1277960 | tf_op jit(solution)/shard_map/ppermute | solution.py:40
  91.2 10.4 %collective-permute-done.7 = f32[2,16,3584]{2,1,0:T(8,128)S(1)} collective-permute-done((f32[2,16,3584]{2,1,0:T(8,128)S(1)}, f32[2,16,3584]{2,1,0:T(8,128)S(1)}, u32[]{:S(2)}, u32[]{:S(2)}) %collective-permute-start.7) | collective-permute-done | bytes 458784 | tf_op jit(solution)/shard_map/ppermute | solution.py:40
  101.6 2.0 collective-permute-done.11
  103.5 1.1 fusion.9
  104.6 6.1 %collective-permute-done.13 = f32[2,16,3328]{2,1,0:T(8,128)S(1)} collective-permute-done((f32[2,16,3328]{2,1,0:T(8,128)S(1)}, f32[2,16,3328]{2,1,0:T(8,128)S(1)}, u32[]{:S(2)}, u32[]{:S(2)}) %collective-permute-start.13) | collective-permute-done | bytes 426016 | tf_op jit(solution)/shard_map/ppermute | solution.py:40
  110.7 2.0 collective-permute-done.14
  112.6 1.1 fusion.10
  113.7 1.9 collective-permute-start.15
  115.7 9.7 %collective-permute-start.12 = (f32[16,3584]{1,0:T(8,128)S(1)}, f32[16,3584]{1,0:T(8,128)S(1)}, u32[]{:S(2)}, u32[]{:S(2)}) collective-permute-start(f32[16,3584]{1,0:T(8,128)S(1)} %select_bitcast_fusion), channel_id=1, source_target_pairs={{0,32},{32,0},{1,33},{33,1},{2,34},{34,2},{3,35},{35,3},{4,36},{36... | collective-permute-start | bytes 688136 | tf_op jit(solution)/shard_map/ppermute | solution.py:40
  125.4 1.2 collective-permute-done.15
  126.8 2.4 %collective-permute-done.12 = f32[16,3584]{1,0:T(8,128)S(1)} collective-permute-done((f32[16,3584]{1,0:T(8,128)S(1)}, f32[16,3584]{1,0:T(8,128)S(1)}, u32[]{:S(2)}, u32[]{:S(2)}) %collective-permute-start.12) | collective-permute-done | bytes 229408 | tf_op jit(solution)/shard_map/ppermute | solution.py:40
  129.2 0.2 multiply_reduce_fusion.1
  129.6 0.6 broadcast_in_dim.10
  130.2 38.0 %all-to-all-start.1 = ((f32[24,1,128]{2,1,0:T(1,128)}), f32[24,1,128]{2,1,0:T(1,128)S(1)}, u32[]{:S(2)}, u32[]{:S(2)}) async-start(f32[24,1,128]{2,1,0:T(1,128)} %broadcast_in_dim.10), calls=%async_computation.1 | async-start | bytes 24576 | tf_op jit(solution)/shard_map/all_to_all | solution.py:17
  168.3 9.3 %all-to-all-done.1 = f32[24,1,128]{2,1,0:T(1,128)S(1)} async-done(((f32[24,1,128]{2,1,0:T(1,128)}), f32[24,1,128]{2,1,0:T(1,128)S(1)}, u32[]{:S(2)}, u32[]{:S(2)}) %all-to-all-start.1) | async-done | bytes 12320 | tf_op jit(solution)/shard_map/all_to_all | solution.py:17
  177.6 0.5 broadcast.74
  178.2 0.7 reduce.9
  179.2 0.6 broadcast_in_dim.11
  179.8 9.3 %all-to-all-start.2 = ((f32[32,1,128]{2,1,0:T(1,128)}), f32[32,1,128]{2,1,0:T(1,128)S(1)}, u32[]{:S(2)}, u32[]{:S(2)}) async-start(f32[32,1,128]{2,1,0:T(1,128)} %broadcast_in_dim.11), calls=%async_computation.2 | async-start | bytes 32768 | tf_op jit(solution)/shard_map/all_to_all | solution.py:17
  189.1 8.7 %all-to-all-done.2 = f32[32,1,128]{2,1,0:T(1,128)S(1)} async-done(((f32[32,1,128]{2,1,0:T(1,128)}), f32[32,1,128]{2,1,0:T(1,128)S(1)}, u32[]{:S(2)}, u32[]{:S(2)}) %all-to-all-start.2) | async-done | bytes 16416 | tf_op jit(solution)/shard_map/all_to_all | solution.py:17
  198.1 0.6 sub.18
  (57 shorter events, 1.9 us)
Async XLA Ops:
  0.0 1.0 copy-start
  1.0 12.2 %copy-start.4 = (bf16[1,8192]{1,0:T(2,128)(2,1)S(1)}, bf16[1,8192]{1,0:T(2,128)(2,1)}, u32[]{:S(2)}) copy-start(bf16[1,8192]{1,0:T(2,128)(2,1)} %param.8) | copy-start | bytes 49156
  5.3 12.1 %collective-permute-start = (f32[16,6912]{1,0:T(8,128)S(1)}, f32[16,6912]{1,0:T(8,128)S(1)}, u32[]{:S(2)}, u32[]{:S(2)}) collective-permute-start(f32[16,6912]{1,0:T(8,128)S(1)} %get-tuple-element.45), channel_id=1, source_target_pairs={{0,4},{4,8},{8,12},{12,16},{16,20},{20,24},{24,28},{28,0},{1,5},{5... | collective-permute-start | bytes 1327112 | tf_op jit(solution)/shard_map/ppermute | solution.py:40
  9.4 9.0 %collective-permute-start.2 = (f32[16,6912]{1,0:T(8,128)S(1)}, f32[16,6912]{1,0:T(8,128)S(1)}, u32[]{:S(2)}, u32[]{:S(2)}) collective-permute-start(f32[16,6912]{1,0:T(8,128)S(1)} %get-tuple-element.46), channel_id=1, source_target_pairs={{0,28},{4,0},{8,4},{12,8},{16,12},{20,16},{24,20},{28,24},{1,29},{... | collective-permute-start | bytes 1327112 | tf_op jit(solution)/shard_map/ppermute | solution.py:40
  14.1 13.2 %copy-start.1 = (bf16[1,512,8192]{2,1,0:T(8,128)(2,1)S(1)}, bf16[1,512,8192]{2,1,0:T(8,128)(2,1)}, u32[]{:S(2)}) copy-start(bf16[1,512,8192]{2,1,0:T(8,128)(2,1)} %param.7) | copy-start | bytes 25165828
  17.4 37.4 %copy-start.2 = (f32[256,3584]{1,0:T(8,128)}, f32[256,3584]{1,0:T(8,128)S(1)}, u32[]{:S(2)}) copy-start(f32[256,3584]{1,0:T(8,128)S(1)} %fusion.2) | copy-start | bytes 11010052
  18.5 36.3 %collective-permute-start.6 = (f32[2,16,3584]{2,1,0:T(8,128)S(1)}, f32[2,16,3584]{2,1,0:T(8,128)S(1)}, u32[]{:S(2)}, u32[]{:S(2)}) collective-permute-start(f32[2,16,3584]{2,1,0:T(8,128)S(1)} %bitcast_add_fusion.3), channel_id=1, source_target_pairs={{0,28},{4,0},{8,4},{12,8},{16,12},{20,16},{24,20},{28,24},{1,29},{... | collective-permute-start | bytes 1376264 | tf_op jit(solution)/shard_map/ppermute | solution.py:40
  24.4 28.2 %collective-permute-start.1 = (f32[2,16,3584]{2,1,0:T(8,128)S(1)}, f32[2,16,3584]{2,1,0:T(8,128)S(1)}, u32[]{:S(2)}, u32[]{:S(2)}) collective-permute-start(f32[2,16,3584]{2,1,0:T(8,128)S(1)} %bitcast_add_fusion.4), channel_id=1, source_target_pairs={{0,4},{4,8},{8,12},{12,16},{16,20},{20,24},{24,28},{28,0},{1,5},{5... | collective-permute-start | bytes 1376264 | tf_op jit(solution)/shard_map/ppermute | solution.py:40
  27.9 38.7 %collective-permute-start.16 = (f32[8,16,1280]{2,1,0:T(8,128)S(1)}, f32[8,16,1280]{2,1,0:T(8,128)S(1)}, u32[]{:S(2)}, u32[]{:S(2)}) collective-permute-start(f32[8,16,1280]{2,1,0:T(8,128)S(1)} %fusion.8), channel_id=1, source_target_pairs={{0,32},{32,0},{1,33},{33,1},{2,34},{34,2},{3,35},{35,3},{4,36},{36... | collective-permute-start | bytes 1966088 | tf_op jit(solution)/shard_map/ppermute | solution.py:40
  45.9 16.4 %copy-start.3 = (f32[256,3328]{1,0:T(8,128)}, f32[256,3328]{1,0:T(8,128)S(1)}, u32[]{:S(2)}) copy-start(f32[256,3328]{1,0:T(8,128)S(1)} %fusion.4) | copy-start | bytes 10223620
  46.0 13.2 %collective-permute-start.5 = (f32[2,16,3328]{2,1,0:T(8,128)S(1)}, f32[2,16,3328]{2,1,0:T(8,128)S(1)}, u32[]{:S(2)}, u32[]{:S(2)}) collective-permute-start(f32[2,16,3328]{2,1,0:T(8,128)S(1)} %bitcast_add_fusion.13), channel_id=1, source_target_pairs={{0,4},{4,8},{8,12},{12,16},{16,20},{20,24},{24,28},{28,0},{1,5},{5... | collective-permute-start | bytes 1277960 | tf_op jit(solution)/shard_map/ppermute | solution.py:40
  48.5 13.0 %collective-permute-start.4 = (f32[2,16,3328]{2,1,0:T(8,128)S(1)}, f32[2,16,3328]{2,1,0:T(8,128)S(1)}, u32[]{:S(2)}, u32[]{:S(2)}) collective-permute-start(f32[2,16,3328]{2,1,0:T(8,128)S(1)} %bitcast_add_fusion.14), channel_id=1, source_target_pairs={{0,28},{4,0},{8,4},{12,8},{16,12},{20,16},{24,20},{28,24},{1,29},{... | collective-permute-start | bytes 1277960 | tf_op jit(solution)/shard_map/ppermute | solution.py:40
  52.6 20.9 %collective-permute-start.3 = (f32[2,16,3584]{2,1,0:T(8,128)S(1)}, f32[2,16,3584]{2,1,0:T(8,128)S(1)}, u32[]{:S(2)}, u32[]{:S(2)}) collective-permute-start(f32[2,16,3584]{2,1,0:T(8,128)S(1)} %bitcast_add_fusion.5), channel_id=1, source_target_pairs={{0,4},{4,8},{8,12},{12,16},{16,20},{20,24},{24,28},{28,0},{1,5},{5... | collective-permute-start | bytes 1376264 | tf_op jit(solution)/shard_map/ppermute | solution.py:40
  54.9 23.1 %collective-permute-start.10 = (f32[2,16,3584]{2,1,0:T(8,128)S(1)}, f32[2,16,3584]{2,1,0:T(8,128)S(1)}, u32[]{:S(2)}, u32[]{:S(2)}) collective-permute-start(f32[2,16,3584]{2,1,0:T(8,128)S(1)} %bitcast_add_fusion.2), channel_id=1, source_target_pairs={{0,28},{4,0},{8,4},{12,8},{16,12},{20,16},{24,20},{28,24},{1,29},{... | collective-permute-start | bytes 1376264 | tf_op jit(solution)/shard_map/ppermute | solution.py:40
  59.3 23.0 %collective-permute-start.9 = (f32[2,16,3328]{2,1,0:T(8,128)S(1)}, f32[2,16,3328]{2,1,0:T(8,128)}, u32[]{:S(2)}, u32[]{:S(2)}) collective-permute-start(f32[2,16,3328]{2,1,0:T(8,128)S(1)} %bitcast_add_fusion.11), channel_id=1, source_target_pairs={{0,4},{4,8},{8,12},{12,16},{16,20},{20,24},{24,28},{28,0},{1,5},{5... | collective-permute-start | bytes 1277960 | tf_op jit(solution)/shard_map/ppermute | solution.py:40
  62.3 23.3 %collective-permute-start.8 = (f32[2,16,3328]{2,1,0:T(8,128)}, f32[2,16,3328]{2,1,0:T(8,128)}, u32[]{:S(2)}, u32[]{:S(2)}) collective-permute-start(f32[2,16,3328]{2,1,0:T(8,128)} %bitcast_add_fusion.12), channel_id=1, source_target_pairs={{0,28},{4,0},{8,4},{12,8},{16,12},{20,16},{24,20},{28,24},{1,29},{... | collective-permute-start | bytes 1277960 | tf_op jit(solution)/shard_map/ppermute | solution.py:40
  67.5 61.9 %all-to-all-start = ((f32[8,16,1280]{2,1,0:T(8,128)}), f32[8,16,1280]{2,1,0:T(8,128)S(1)}, u32[]{:S(2)}, u32[]{:S(2)}) async-start(f32[8,16,1280]{2,1,0:T(8,128)} %bitcast_add_fusion), calls=%async_computation | async-start | bytes 1310720 | tf_op jit(solution)/shard_map/all_to_all | solution.py:103
  74.6 26.9 %collective-permute-start.7 = (f32[2,16,3584]{2,1,0:T(8,128)S(1)}, f32[2,16,3584]{2,1,0:T(8,128)S(1)}, u32[]{:S(2)}, u32[]{:S(2)}) collective-permute-start(f32[2,16,3584]{2,1,0:T(8,128)S(1)} %bitcast_add_fusion.6), channel_id=1, source_target_pairs={{0,4},{4,8},{8,12},{12,16},{16,20},{20,24},{24,28},{28,0},{1,5},{5... | collective-permute-start | bytes 1376264 | tf_op jit(solution)/shard_map/ppermute | solution.py:40
  79.1 24.4 %collective-permute-start.11 = (f32[2,16,3584]{2,1,0:T(8,128)S(1)}, f32[2,16,3584]{2,1,0:T(8,128)S(1)}, u32[]{:S(2)}, u32[]{:S(2)}) collective-permute-start(f32[2,16,3584]{2,1,0:T(8,128)S(1)} %bitcast_add_fusion.1), channel_id=1, source_target_pairs={{0,28},{4,0},{8,4},{12,8},{16,12},{20,16},{24,20},{28,24},{1,29},{... | collective-permute-start | bytes 1376264 | tf_op jit(solution)/shard_map/ppermute | solution.py:40
  83.4 27.2 %collective-permute-start.13 = (f32[2,16,3328]{2,1,0:T(8,128)S(1)}, f32[2,16,3328]{2,1,0:T(8,128)S(1)}, u32[]{:S(2)}, u32[]{:S(2)}) collective-permute-start(f32[2,16,3328]{2,1,0:T(8,128)S(1)} %bitcast_add_fusion.9), channel_id=1, source_target_pairs={{0,4},{4,8},{8,12},{12,16},{16,20},{20,24},{24,28},{28,0},{1,5},{5... | collective-permute-start | bytes 1277960 | tf_op jit(solution)/shard_map/ppermute | solution.py:40
  86.8 81.4 %copy-start.5 = (s32[256,1]{0,1:T(1,128)S(1)}, s32[256,1]{0,1:T(1,128)}, u32[]{:S(2)}) copy-start(s32[256,1]{0,1:T(1,128)} %param.6) | copy-start | bytes 3076
  86.8 25.8 %collective-permute-start.14 = (f32[2,16,3328]{2,1,0:T(8,128)S(1)}, f32[2,16,3328]{2,1,0:T(8,128)S(1)}, u32[]{:S(2)}, u32[]{:S(2)}) collective-permute-start(f32[2,16,3328]{2,1,0:T(8,128)S(1)} %bitcast_add_fusion.10), channel_id=1, source_target_pairs={{0,28},{4,0},{8,4},{12,8},{16,12},{20,16},{24,20},{28,24},{1,29},{... | collective-permute-start | bytes 1277960 | tf_op jit(solution)/shard_map/ppermute | solution.py:40
  113.7 12.9 %collective-permute-start.15 = (f32[16,3328]{1,0:T(8,128)S(1)}, f32[16,3328]{1,0:T(8,128)S(1)}, u32[]{:S(2)}, u32[]{:S(2)}) collective-permute-start(f32[16,3328]{1,0:T(8,128)S(1)} %select_bitcast_fusion.1), channel_id=1, source_target_pairs={{0,32},{32,0},{1,33},{33,1},{2,34},{34,2},{3,35},{35,3},{4,36},{36... | collective-permute-start | bytes 638984 | tf_op jit(solution)/shard_map/ppermute | solution.py:40
  115.7 13.5 %collective-permute-start.12 = (f32[16,3584]{1,0:T(8,128)S(1)}, f32[16,3584]{1,0:T(8,128)S(1)}, u32[]{:S(2)}, u32[]{:S(2)}) collective-permute-start(f32[16,3584]{1,0:T(8,128)S(1)} %select_bitcast_fusion), channel_id=1, source_target_pairs={{0,32},{32,0},{1,33},{33,1},{2,34},{34,2},{3,35},{35,3},{4,36},{36... | collective-permute-start | bytes 688136 | tf_op jit(solution)/shard_map/ppermute | solution.py:40
  130.2 47.4 %all-to-all-start.1 = ((f32[24,1,128]{2,1,0:T(1,128)}), f32[24,1,128]{2,1,0:T(1,128)S(1)}, u32[]{:S(2)}, u32[]{:S(2)}) async-start(f32[24,1,128]{2,1,0:T(1,128)} %broadcast_in_dim.10), calls=%async_computation.1 | async-start | bytes 24576 | tf_op jit(solution)/shard_map/all_to_all | solution.py:17
  179.8 17.9 %all-to-all-start.2 = ((f32[32,1,128]{2,1,0:T(1,128)}), f32[32,1,128]{2,1,0:T(1,128)S(1)}, u32[]{:S(2)}, u32[]{:S(2)}) async-start(f32[32,1,128]{2,1,0:T(1,128)} %broadcast_in_dim.11), calls=%async_computation.2 | async-start | bytes 32768 | tf_op jit(solution)/shard_map/all_to_all | solution.py:17

commit v4 on v3

--- a/solution.py
+++ b/solution.py
@@ -112,8 +112,9 @@
     pair = ZH * own
     pair_target = lax.dynamic_slice_in_dim(target, y * pair, pair)
     pair_member = (pair_target[:, None] == names).astype(jnp.float32)
-    scores = everyone(score, ("zh", "section")).reshape(ZH, -1, LANES)
-    combined = jnp.sum(scores, axis=1)[:, :own].reshape(pair)
+    scores = everyone(score, ("zh", "section"))
+    side = jnp.arange(scores.shape[0])[:, None] // (scores.shape[0] // ZH)
+    combined = jnp.concatenate([jnp.sum(jnp.where(side == z, scores, 0.0), axis=0)[:own] for z in range(ZH)])
     totals = jnp.sum(pair_member * combined[:, None], axis=0)
     counts = jnp.sum(pair_member, axis=0)
     pieces = everyone(jnp.concatenate([combined, totals, counts]), ("dp", "y")).reshape(groups, ring, LANES)

time: 200 us -> 198 us (0.990)
  no operation moved by 1% of the time
where the time goes in v4:
time: 198 us; the launch traced here: 197 us
  starting transfers between devices  131 us (66%)
  waiting for transfers between devices  42.9 us (22%)
  other arithmetic  10.7 us (5%)
  matrix products  9.18 us (5%)
  local copies, waits for them, and re-layouts  2.59 us (1%)
    ppermute x17, starting transfers between devices, ship(): return lax.ppermute(value, axis, pairs)  77.6 us
    all_to_all x2, starting transfers between devices, everyone(): return lax.all_to_all(copies, axes, 0, 0, tiled=True)  47.3 us
    ppermute x17, waiting for transfers between devices, ship(): return lax.ppermute(value, axis, pairs)  24.9 us
    all_to_all x2, waiting for transfers between devices, everyone(): return lax.all_to_all(copies, axes, 0, 0, tiled=True)  18 us
    add x14, other arithmetic, join(): total = total + value  7.83 us
    all_to_all x1, starting transfers between devices, body(): turned = lax.all_to_all(z_summed, 'y', 0, 0, tiled=True)  6.02 us
    dot_general x2, matrix products, group_product(): jnp.dot(after_last(rows), matrix[:, cuts[g]:cuts[g + 1]], preferred_eleme...  4.35 us
    dot_general x1, matrix products, body(): jnp.dot(opposite_rows, matrix[:, :columns], preferred_element_type=jnp.fl...  4.32 us
  transfers between devices with their start and end apart: 20, of which 9 were waited for; matrix products, arithmetic and copies ran while one was open for 7% of the time, Pallas kernels for 0%

profile of v4, /device:TPU:1, one launch (start us, length us, event | category | flops | bytes accessed | tf_op | source)
XLA Modules:
  0.0 197.5 jit_solution(16121615366357923836)
XLA Ops:
  0.0 0.9 copy-done
  1.0 4.3 %fusion = f32[32,6912]{1,0:T(8,128)S(1)} fusion(bf16[512,8192]{1,0:T(8,128)(2,1)} %bitcast.82, bf16[1,256,512]{2,1,0:T(8,128)(2,1)S(1)} %copy-done, s32[]{:T(128)S(6)} %select_n.168), kind=kOutput, calls=%fused_computation | convolution fusion | flops 226492416 | bytes 7995396 | tf_op jit(solution)/shard_map/dot_general | solution.py:59
  5.3 4.0 %collective-permute-start = (f32[16,6912]{1,0:T(8,128)S(1)}, f32[16,6912]{1,0:T(8,128)S(1)}, u32[]{:S(2)}, u32[]{:S(2)}) collective-permute-start(f32[16,6912]{1,0:T(8,128)S(1)} %get-tuple-element.47), channel_id=1, source_target_pairs={{0,4},{4,8},{8,12},{12,16},{16,20},{20,24},{24,28},{28,0},{1,5},{5... | collective-permute-start | bytes 1327112 | tf_op jit(solution)/shard_map/ppermute | solution.py:40
  9.4 3.8 %collective-permute-start.2 = (f32[16,6912]{1,0:T(8,128)S(1)}, f32[16,6912]{1,0:T(8,128)S(1)}, u32[]{:S(2)}, u32[]{:S(2)}) collective-permute-start(f32[16,6912]{1,0:T(8,128)S(1)} %get-tuple-element.48), channel_id=1, source_target_pairs={{0,28},{4,0},{8,4},{12,8},{16,12},{20,16},{24,20},{28,24},{1,29},{... | collective-permute-start | bytes 1327112 | tf_op jit(solution)/shard_map/ppermute | solution.py:40
  14.1 3.3 %fusion.2 = f32[256,3584]{1,0:T(8,128)S(1)} fusion(bf16[256,512]{1,0:T(8,128)(2,1)S(1)} %bitcast.79, bf16[512,8192]{1,0:T(8,128)(2,1)} %bitcast.83), kind=kOutput, calls=%fused_computation.2 | convolution fusion | flops 939524096 | bytes 7602176 | tf_op jit(solution)/shard_map/dot_general | solution.py:64
  17.5 0.9 collective-permute-done.2
  18.5 5.9 %collective-permute-start.6 = (f32[2,16,3584]{2,1,0:T(8,128)S(1)}, f32[2,16,3584]{2,1,0:T(8,128)S(1)}, u32[]{:S(2)}, u32[]{:S(2)}) collective-permute-start(f32[2,16,3584]{2,1,0:T(8,128)S(1)} %bitcast_add_fusion.3), channel_id=1, source_target_pairs={{0,28},{4,0},{8,4},{12,8},{16,12},{20,16},{24,20},{28,24},{1,29},{... | collective-permute-start | bytes 1376264 | tf_op jit(solution)/shard_map/ppermute | solution.py:40
  24.4 2.9 %collective-permute-start.1 = (f32[2,16,3584]{2,1,0:T(8,128)S(1)}, f32[2,16,3584]{2,1,0:T(8,128)S(1)}, u32[]{:S(2)}, u32[]{:S(2)}) collective-permute-start(f32[2,16,3584]{2,1,0:T(8,128)S(1)} %bitcast_add_fusion.4), channel_id=1, source_target_pairs={{0,4},{4,8},{8,12},{12,16},{16,20},{20,24},{24,28},{28,0},{1,5},{5... | collective-permute-start | bytes 1376264 | tf_op jit(solution)/shard_map/ppermute | solution.py:40
  27.3 0.5 fusion.6
  27.9 17.0 %collective-permute-start.16 = (f32[8,16,1280]{2,1,0:T(8,128)S(1)}, f32[8,16,1280]{2,1,0:T(8,128)S(1)}, u32[]{:S(2)}, u32[]{:S(2)}) collective-permute-start(f32[8,16,1280]{2,1,0:T(8,128)S(1)} %fusion.8), channel_id=1, source_target_pairs={{0,32},{32,0},{1,33},{33,1},{2,34},{34,2},{3,35},{35,3},{4,36},{36... | collective-permute-start | bytes 1966088 | tf_op jit(solution)/shard_map/ppermute | solution.py:40
  44.8 1.1 fusion.4
  46.0 2.4 %collective-permute-start.5 = (f32[2,16,3328]{2,1,0:T(8,128)S(1)}, f32[2,16,3328]{2,1,0:T(8,128)S(1)}, u32[]{:S(2)}, u32[]{:S(2)}) collective-permute-start(f32[2,16,3328]{2,1,0:T(8,128)S(1)} %bitcast_add_fusion.13), channel_id=1, source_target_pairs={{0,4},{4,8},{8,12},{12,16},{16,20},{20,24},{24,28},{28,0},{1,5},{5... | collective-permute-start | bytes 1277960 | tf_op jit(solution)/shard_map/ppermute | solution.py:40
  48.5 4.1 %collective-permute-start.4 = (f32[2,16,3328]{2,1,0:T(8,128)S(1)}, f32[2,16,3328]{2,1,0:T(8,128)S(1)}, u32[]{:S(2)}, u32[]{:S(2)}) collective-permute-start(f32[2,16,3328]{2,1,0:T(8,128)S(1)} %bitcast_add_fusion.14), channel_id=1, source_target_pairs={{0,28},{4,0},{8,4},{12,8},{16,12},{20,16},{24,20},{28,24},{1,29},{... | collective-permute-start | bytes 1277960 | tf_op jit(solution)/shard_map/ppermute | solution.py:40
  52.6 2.2 %collective-permute-start.3 = (f32[2,16,3584]{2,1,0:T(8,128)S(1)}, f32[2,16,3584]{2,1,0:T(8,128)S(1)}, u32[]{:S(2)}, u32[]{:S(2)}) collective-permute-start(f32[2,16,3584]{2,1,0:T(8,128)S(1)} %bitcast_add_fusion.5), channel_id=1, source_target_pairs={{0,4},{4,8},{8,12},{12,16},{16,20},{20,24},{24,28},{28,0},{1,5},{5... | collective-permute-start | bytes 1376264 | tf_op jit(solution)/shard_map/ppermute | solution.py:40
  54.9 4.3 %collective-permute-start.10 = (f32[2,16,3584]{2,1,0:T(8,128)S(1)}, f32[2,16,3584]{2,1,0:T(8,128)S(1)}, u32[]{:S(2)}, u32[]{:S(2)}) collective-permute-start(f32[2,16,3584]{2,1,0:T(8,128)S(1)} %bitcast_add_fusion.2), channel_id=1, source_target_pairs={{0,28},{4,0},{8,4},{12,8},{16,12},{20,16},{24,20},{28,24},{1,29},{... | collective-permute-start | bytes 1376264 | tf_op jit(solution)/shard_map/ppermute | solution.py:40
  59.3 2.2 %collective-permute-start.9 = (f32[2,16,3328]{2,1,0:T(8,128)S(1)}, f32[2,16,3328]{2,1,0:T(8,128)}, u32[]{:S(2)}, u32[]{:S(2)}) collective-permute-start(f32[2,16,3328]{2,1,0:T(8,128)S(1)} %bitcast_add_fusion.11), channel_id=1, source_target_pairs={{0,4},{4,8},{8,12},{12,16},{16,20},{20,24},{24,28},{28,0},{1,5},{5... | collective-permute-start | bytes 1277960 | tf_op jit(solution)/shard_map/ppermute | solution.py:40
  61.5 0.8 bitcast_add_fusion.12
  62.3 4.3 %collective-permute-start.8 = (f32[2,16,3328]{2,1,0:T(8,128)}, f32[2,16,3328]{2,1,0:T(8,128)}, u32[]{:S(2)}, u32[]{:S(2)}) collective-permute-start(f32[2,16,3328]{2,1,0:T(8,128)} %bitcast_add_fusion.12), channel_id=1, source_target_pairs={{0,28},{4,0},{8,4},{12,8},{16,12},{20,16},{24,20},{28,24},{1,29},{... | collective-permute-start | bytes 1277960 | tf_op jit(solution)/shard_map/ppermute | solution.py:40
  66.6 0.9 bitcast_add_fusion
  67.5 6.0 %all-to-all-start = ((f32[8,16,1280]{2,1,0:T(8,128)}), f32[8,16,1280]{2,1,0:T(8,128)S(1)}, u32[]{:S(2)}, u32[]{:S(2)}) async-start(f32[8,16,1280]{2,1,0:T(8,128)} %bitcast_add_fusion), calls=%async_computation | async-start | bytes 1310720 | tf_op jit(solution)/shard_map/all_to_all | solution.py:103
  73.6 1.1 bitcast_add_fusion.6
  74.6 3.4 %collective-permute-start.7 = (f32[2,16,3584]{2,1,0:T(8,128)S(1)}, f32[2,16,3584]{2,1,0:T(8,128)S(1)}, u32[]{:S(2)}, u32[]{:S(2)}) collective-permute-start(f32[2,16,3584]{2,1,0:T(8,128)S(1)} %bitcast_add_fusion.6), channel_id=1, source_target_pairs={{0,4},{4,8},{8,12},{12,16},{16,20},{20,24},{24,28},{28,0},{1,5},{5... | collective-permute-start | bytes 1376264 | tf_op jit(solution)/shard_map/ppermute | solution.py:40
  78.0 1.1 bitcast_add_fusion.1
  79.1 3.1 %collective-permute-start.11 = (f32[2,16,3584]{2,1,0:T(8,128)S(1)}, f32[2,16,3584]{2,1,0:T(8,128)S(1)}, u32[]{:S(2)}, u32[]{:S(2)}) collective-permute-start(f32[2,16,3584]{2,1,0:T(8,128)S(1)} %bitcast_add_fusion.1), channel_id=1, source_target_pairs={{0,28},{4,0},{8,4},{12,8},{16,12},{20,16},{24,20},{28,24},{1,29},{... | collective-permute-start | bytes 1376264 | tf_op jit(solution)/shard_map/ppermute | solution.py:40
  82.3 1.2 bitcast_add_fusion.9
  83.4 2.1 %collective-permute-start.13 = (f32[2,16,3328]{2,1,0:T(8,128)S(1)}, f32[2,16,3328]{2,1,0:T(8,128)S(1)}, u32[]{:S(2)}, u32[]{:S(2)}) collective-permute-start(f32[2,16,3328]{2,1,0:T(8,128)S(1)} %bitcast_add_fusion.9), channel_id=1, source_target_pairs={{0,4},{4,8},{8,12},{12,16},{16,20},{20,24},{24,28},{28,0},{1,5},{5... | collective-permute-start | bytes 1277960 | tf_op jit(solution)/shard_map/ppermute | solution.py:40
  85.6 1.2 bitcast_add_fusion.10
  86.8 4.3 %collective-permute-start.14 = (f32[2,16,3328]{2,1,0:T(8,128)S(1)}, f32[2,16,3328]{2,1,0:T(8,128)S(1)}, u32[]{:S(2)}, u32[]{:S(2)}) collective-permute-start(f32[2,16,3328]{2,1,0:T(8,128)S(1)} %bitcast_add_fusion.10), channel_id=1, source_target_pairs={{0,28},{4,0},{8,4},{12,8},{16,12},{20,16},{24,20},{28,24},{1,29},{... | collective-permute-start | bytes 1277960 | tf_op jit(solution)/shard_map/ppermute | solution.py:40
  91.2 10.4 %collective-permute-done.7 = f32[2,16,3584]{2,1,0:T(8,128)S(1)} collective-permute-done((f32[2,16,3584]{2,1,0:T(8,128)S(1)}, f32[2,16,3584]{2,1,0:T(8,128)S(1)}, u32[]{:S(2)}, u32[]{:S(2)}) %collective-permute-start.7) | collective-permute-done | bytes 458784 | tf_op jit(solution)/shard_map/ppermute | solution.py:40
  101.6 2.0 collective-permute-done.11
  103.5 1.1 fusion.9
  104.6 6.1 %collective-permute-done.13 = f32[2,16,3328]{2,1,0:T(8,128)S(1)} collective-permute-done((f32[2,16,3328]{2,1,0:T(8,128)S(1)}, f32[2,16,3328]{2,1,0:T(8,128)S(1)}, u32[]{:S(2)}, u32[]{:S(2)}) %collective-permute-start.13) | collective-permute-done | bytes 426016 | tf_op jit(solution)/shard_map/ppermute | solution.py:40
  110.7 2.0 collective-permute-done.14
  112.6 1.1 fusion.10
  113.7 1.9 collective-permute-start.15
  115.7 9.7 %collective-permute-start.12 = (f32[16,3584]{1,0:T(8,128)S(1)}, f32[16,3584]{1,0:T(8,128)S(1)}, u32[]{:S(2)}, u32[]{:S(2)}) collective-permute-start(f32[16,3584]{1,0:T(8,128)S(1)} %select_bitcast_fusion), channel_id=1, source_target_pairs={{0,32},{32,0},{1,33},{33,1},{2,34},{34,2},{3,35},{35,3},{4,36},{36... | collective-permute-start | bytes 688136 | tf_op jit(solution)/shard_map/ppermute | solution.py:40
  125.4 1.2 collective-permute-done.15
  126.6 0.2 multiply_reduce_fusion.3
  126.8 2.4 %collective-permute-done.12 = f32[16,3584]{1,0:T(8,128)S(1)} collective-permute-done((f32[16,3584]{1,0:T(8,128)S(1)}, f32[16,3584]{1,0:T(8,128)S(1)}, u32[]{:S(2)}, u32[]{:S(2)}) %collective-permute-start.12) | collective-permute-done | bytes 229408 | tf_op jit(solution)/shard_map/ppermute | solution.py:40
  129.2 0.2 multiply_reduce_fusion.1
  129.6 0.6 broadcast_in_dim.47
  130.2 38.0 %all-to-all-start.1 = ((f32[24,1,128]{2,1,0:T(1,128)}), f32[24,1,128]{2,1,0:T(1,128)S(1)}, u32[]{:S(2)}, u32[]{:S(2)}) async-start(f32[24,1,128]{2,1,0:T(1,128)} %broadcast_in_dim.47), calls=%async_computation.1 | async-start | bytes 24576 | tf_op jit(solution)/shard_map/all_to_all | solution.py:17
  168.3 9.3 %all-to-all-done.1 = f32[24,1,128]{2,1,0:T(1,128)S(1)} async-done(((f32[24,1,128]{2,1,0:T(1,128)}), f32[24,1,128]{2,1,0:T(1,128)S(1)}, u32[]{:S(2)}, u32[]{:S(2)}) %all-to-all-start.1) | async-done | bytes 12320 | tf_op jit(solution)/shard_map/all_to_all | solution.py:17
  177.8 0.1 select_reduce_fusion.3
  178.1 0.6 broadcast_in_dim.50
  178.7 9.2 %all-to-all-start.2 = ((f32[32,1,128]{2,1,0:T(1,128)}), f32[32,1,128]{2,1,0:T(1,128)S(1)}, u32[]{:S(2)}, u32[]{:S(2)}) async-start(f32[32,1,128]{2,1,0:T(1,128)} %broadcast_in_dim.50), calls=%async_computation.2 | async-start | bytes 32768 | tf_op jit(solution)/shard_map/all_to_all | solution.py:17
  187.9 8.7 %all-to-all-done.2 = f32[32,1,128]{2,1,0:T(1,128)S(1)} async-done(((f32[32,1,128]{2,1,0:T(1,128)}), f32[32,1,128]{2,1,0:T(1,128)S(1)}, u32[]{:S(2)}, u32[]{:S(2)}) %all-to-all-start.2) | async-done | bytes 16416 | tf_op jit(solution)/shard_map/all_to_all | solution.py:17
  196.9 0.6 sub.25
  (55 shorter events, 1.6 us)
Async XLA Ops:
  0.0 1.0 copy-start
  1.0 12.2 %copy-start.4 = (bf16[1,8192]{1,0:T(2,128)(2,1)S(1)}, bf16[1,8192]{1,0:T(2,128)(2,1)}, u32[]{:S(2)}) copy-start(bf16[1,8192]{1,0:T(2,128)(2,1)} %param.8) | copy-start | bytes 49156
  5.3 12.1 %collective-permute-start = (f32[16,6912]{1,0:T(8,128)S(1)}, f32[16,6912]{1,0:T(8,128)S(1)}, u32[]{:S(2)}, u32[]{:S(2)}) collective-permute-start(f32[16,6912]{1,0:T(8,128)S(1)} %get-tuple-element.47), channel_id=1, source_target_pairs={{0,4},{4,8},{8,12},{12,16},{16,20},{20,24},{24,28},{28,0},{1,5},{5... | collective-permute-start | bytes 1327112 | tf_op jit(solution)/shard_map/ppermute | solution.py:40
  9.4 9.0 %collective-permute-start.2 = (f32[16,6912]{1,0:T(8,128)S(1)}, f32[16,6912]{1,0:T(8,128)S(1)}, u32[]{:S(2)}, u32[]{:S(2)}) collective-permute-start(f32[16,6912]{1,0:T(8,128)S(1)} %get-tuple-element.48), channel_id=1, source_target_pairs={{0,28},{4,0},{8,4},{12,8},{16,12},{20,16},{24,20},{28,24},{1,29},{... | collective-permute-start | bytes 1327112 | tf_op jit(solution)/shard_map/ppermute | solution.py:40
  14.1 13.1 %copy-start.1 = (bf16[1,512,8192]{2,1,0:T(8,128)(2,1)S(1)}, bf16[1,512,8192]{2,1,0:T(8,128)(2,1)}, u32[]{:S(2)}) copy-start(bf16[1,512,8192]{2,1,0:T(8,128)(2,1)} %param.7) | copy-start | bytes 25165828
  17.4 37.4 %copy-start.2 = (f32[256,3584]{1,0:T(8,128)}, f32[256,3584]{1,0:T(8,128)S(1)}, u32[]{:S(2)}) copy-start(f32[256,3584]{1,0:T(8,128)S(1)} %fusion.2) | copy-start | bytes 11010052
  18.5 36.3 %collective-permute-start.6 = (f32[2,16,3584]{2,1,0:T(8,128)S(1)}, f32[2,16,3584]{2,1,0:T(8,128)S(1)}, u32[]{:S(2)}, u32[]{:S(2)}) collective-permute-start(f32[2,16,3584]{2,1,0:T(8,128)S(1)} %bitcast_add_fusion.3), channel_id=1, source_target_pairs={{0,28},{4,0},{8,4},{12,8},{16,12},{20,16},{24,20},{28,24},{1,29},{... | collective-permute-start | bytes 1376264 | tf_op jit(solution)/shard_map/ppermute | solution.py:40
  24.4 28.2 %collective-permute-start.1 = (f32[2,16,3584]{2,1,0:T(8,128)S(1)}, f32[2,16,3584]{2,1,0:T(8,128)S(1)}, u32[]{:S(2)}, u32[]{:S(2)}) collective-permute-start(f32[2,16,3584]{2,1,0:T(8,128)S(1)} %bitcast_add_fusion.4), channel_id=1, source_target_pairs={{0,4},{4,8},{8,12},{12,16},{16,20},{20,24},{24,28},{28,0},{1,5},{5... | collective-permute-start | bytes 1376264 | tf_op jit(solution)/shard_map/ppermute | solution.py:40
  27.9 38.7 %collective-permute-start.16 = (f32[8,16,1280]{2,1,0:T(8,128)S(1)}, f32[8,16,1280]{2,1,0:T(8,128)S(1)}, u32[]{:S(2)}, u32[]{:S(2)}) collective-permute-start(f32[8,16,1280]{2,1,0:T(8,128)S(1)} %fusion.8), channel_id=1, source_target_pairs={{0,32},{32,0},{1,33},{33,1},{2,34},{34,2},{3,35},{35,3},{4,36},{36... | collective-permute-start | bytes 1966088 | tf_op jit(solution)/shard_map/ppermute | solution.py:40
  45.9 16.4 %copy-start.3 = (f32[256,3328]{1,0:T(8,128)}, f32[256,3328]{1,0:T(8,128)S(1)}, u32[]{:S(2)}) copy-start(f32[256,3328]{1,0:T(8,128)S(1)} %fusion.4) | copy-start | bytes 10223620
  46.0 13.2 %collective-permute-start.5 = (f32[2,16,3328]{2,1,0:T(8,128)S(1)}, f32[2,16,3328]{2,1,0:T(8,128)S(1)}, u32[]{:S(2)}, u32[]{:S(2)}) collective-permute-start(f32[2,16,3328]{2,1,0:T(8,128)S(1)} %bitcast_add_fusion.13), channel_id=1, source_target_pairs={{0,4},{4,8},{8,12},{12,16},{16,20},{20,24},{24,28},{28,0},{1,5},{5... | collective-permute-start | bytes 1277960 | tf_op jit(solution)/shard_map/ppermute | solution.py:40
  48.5 13.0 %collective-permute-start.4 = (f32[2,16,3328]{2,1,0:T(8,128)S(1)}, f32[2,16,3328]{2,1,0:T(8,128)S(1)}, u32[]{:S(2)}, u32[]{:S(2)}) collective-permute-start(f32[2,16,3328]{2,1,0:T(8,128)S(1)} %bitcast_add_fusion.14), channel_id=1, source_target_pairs={{0,28},{4,0},{8,4},{12,8},{16,12},{20,16},{24,20},{28,24},{1,29},{... | collective-permute-start | bytes 1277960 | tf_op jit(solution)/shard_map/ppermute | solution.py:40
  52.6 20.9 %collective-permute-start.3 = (f32[2,16,3584]{2,1,0:T(8,128)S(1)}, f32[2,16,3584]{2,1,0:T(8,128)S(1)}, u32[]{:S(2)}, u32[]{:S(2)}) collective-permute-start(f32[2,16,3584]{2,1,0:T(8,128)S(1)} %bitcast_add_fusion.5), channel_id=1, source_target_pairs={{0,4},{4,8},{8,12},{12,16},{16,20},{20,24},{24,28},{28,0},{1,5},{5... | collective-permute-start | bytes 1376264 | tf_op jit(solution)/shard_map/ppermute | solution.py:40
  54.9 23.1 %collective-permute-start.10 = (f32[2,16,3584]{2,1,0:T(8,128)S(1)}, f32[2,16,3584]{2,1,0:T(8,128)S(1)}, u32[]{:S(2)}, u32[]{:S(2)}) collective-permute-start(f32[2,16,3584]{2,1,0:T(8,128)S(1)} %bitcast_add_fusion.2), channel_id=1, source_target_pairs={{0,28},{4,0},{8,4},{12,8},{16,12},{20,16},{24,20},{28,24},{1,29},{... | collective-permute-start | bytes 1376264 | tf_op jit(solution)/shard_map/ppermute | solution.py:40
  59.3 23.0 %collective-permute-start.9 = (f32[2,16,3328]{2,1,0:T(8,128)S(1)}, f32[2,16,3328]{2,1,0:T(8,128)}, u32[]{:S(2)}, u32[]{:S(2)}) collective-permute-start(f32[2,16,3328]{2,1,0:T(8,128)S(1)} %bitcast_add_fusion.11), channel_id=1, source_target_pairs={{0,4},{4,8},{8,12},{12,16},{16,20},{20,24},{24,28},{28,0},{1,5},{5... | collective-permute-start | bytes 1277960 | tf_op jit(solution)/shard_map/ppermute | solution.py:40
  62.3 23.3 %collective-permute-start.8 = (f32[2,16,3328]{2,1,0:T(8,128)}, f32[2,16,3328]{2,1,0:T(8,128)}, u32[]{:S(2)}, u32[]{:S(2)}) collective-permute-start(f32[2,16,3328]{2,1,0:T(8,128)} %bitcast_add_fusion.12), channel_id=1, source_target_pairs={{0,28},{4,0},{8,4},{12,8},{16,12},{20,16},{24,20},{28,24},{1,29},{... | collective-permute-start | bytes 1277960 | tf_op jit(solution)/shard_map/ppermute | solution.py:40
  67.5 61.9 %all-to-all-start = ((f32[8,16,1280]{2,1,0:T(8,128)}), f32[8,16,1280]{2,1,0:T(8,128)S(1)}, u32[]{:S(2)}, u32[]{:S(2)}) async-start(f32[8,16,1280]{2,1,0:T(8,128)} %bitcast_add_fusion), calls=%async_computation | async-start | bytes 1310720 | tf_op jit(solution)/shard_map/all_to_all | solution.py:103
  74.6 26.9 %collective-permute-start.7 = (f32[2,16,3584]{2,1,0:T(8,128)S(1)}, f32[2,16,3584]{2,1,0:T(8,128)S(1)}, u32[]{:S(2)}, u32[]{:S(2)}) collective-permute-start(f32[2,16,3584]{2,1,0:T(8,128)S(1)} %bitcast_add_fusion.6), channel_id=1, source_target_pairs={{0,4},{4,8},{8,12},{12,16},{16,20},{20,24},{24,28},{28,0},{1,5},{5... | collective-permute-start | bytes 1376264 | tf_op jit(solution)/shard_map/ppermute | solution.py:40
  79.1 24.4 %collective-permute-start.11 = (f32[2,16,3584]{2,1,0:T(8,128)S(1)}, f32[2,16,3584]{2,1,0:T(8,128)S(1)}, u32[]{:S(2)}, u32[]{:S(2)}) collective-permute-start(f32[2,16,3584]{2,1,0:T(8,128)S(1)} %bitcast_add_fusion.1), channel_id=1, source_target_pairs={{0,28},{4,0},{8,4},{12,8},{16,12},{20,16},{24,20},{28,24},{1,29},{... | collective-permute-start | bytes 1376264 | tf_op jit(solution)/shard_map/ppermute | solution.py:40
  83.4 27.2 %collective-permute-start.13 = (f32[2,16,3328]{2,1,0:T(8,128)S(1)}, f32[2,16,3328]{2,1,0:T(8,128)S(1)}, u32[]{:S(2)}, u32[]{:S(2)}) collective-permute-start(f32[2,16,3328]{2,1,0:T(8,128)S(1)} %bitcast_add_fusion.9), channel_id=1, source_target_pairs={{0,4},{4,8},{8,12},{12,16},{16,20},{20,24},{24,28},{28,0},{1,5},{5... | collective-permute-start | bytes 1277960 | tf_op jit(solution)/shard_map/ppermute | solution.py:40
  86.8 81.4 %copy-start.5 = (s32[256,1]{0,1:T(1,128)S(1)}, s32[256,1]{0,1:T(1,128)}, u32[]{:S(2)}) copy-start(s32[256,1]{0,1:T(1,128)} %param.6) | copy-start | bytes 3076
  86.8 25.8 %collective-permute-start.14 = (f32[2,16,3328]{2,1,0:T(8,128)S(1)}, f32[2,16,3328]{2,1,0:T(8,128)S(1)}, u32[]{:S(2)}, u32[]{:S(2)}) collective-permute-start(f32[2,16,3328]{2,1,0:T(8,128)S(1)} %bitcast_add_fusion.10), channel_id=1, source_target_pairs={{0,28},{4,0},{8,4},{12,8},{16,12},{20,16},{24,20},{28,24},{1,29},{... | collective-permute-start | bytes 1277960 | tf_op jit(solution)/shard_map/ppermute | solution.py:40
  113.7 12.9 %collective-permute-start.15 = (f32[16,3328]{1,0:T(8,128)S(1)}, f32[16,3328]{1,0:T(8,128)S(1)}, u32[]{:S(2)}, u32[]{:S(2)}) collective-permute-start(f32[16,3328]{1,0:T(8,128)S(1)} %select_bitcast_fusion.1), channel_id=1, source_target_pairs={{0,32},{32,0},{1,33},{33,1},{2,34},{34,2},{3,35},{35,3},{4,36},{36... | collective-permute-start | bytes 638984 | tf_op jit(solution)/shard_map/ppermute | solution.py:40
  115.7 13.5 %collective-permute-start.12 = (f32[16,3584]{1,0:T(8,128)S(1)}, f32[16,3584]{1,0:T(8,128)S(1)}, u32[]{:S(2)}, u32[]{:S(2)}) collective-permute-start(f32[16,3584]{1,0:T(8,128)S(1)} %select_bitcast_fusion), channel_id=1, source_target_pairs={{0,32},{32,0},{1,33},{33,1},{2,34},{34,2},{3,35},{35,3},{4,36},{36... | collective-permute-start | bytes 688136 | tf_op jit(solution)/shard_map/ppermute | solution.py:40
  130.2 47.5 %all-to-all-start.1 = ((f32[24,1,128]{2,1,0:T(1,128)}), f32[24,1,128]{2,1,0:T(1,128)S(1)}, u32[]{:S(2)}, u32[]{:S(2)}) async-start(f32[24,1,128]{2,1,0:T(1,128)} %broadcast_in_dim.47), calls=%async_computation.1 | async-start | bytes 24576 | tf_op jit(solution)/shard_map/all_to_all | solution.py:17
  178.7 17.9 %all-to-all-start.2 = ((f32[32,1,128]{2,1,0:T(1,128)}), f32[32,1,128]{2,1,0:T(1,128)S(1)}, u32[]{:S(2)}, u32[]{:S(2)}) async-start(f32[32,1,128]{2,1,0:T(1,128)} %broadcast_in_dim.50), calls=%async_computation.2 | async-start | bytes 32768 | tf_op jit(solution)/shard_map/all_to_all | solution.py:17
